TPU v7x, 128 devices: a whole 4x4x4 slice. The times are simulated.
128 devices in a mesh: row: 4 (over y_hi, core), col: 32 (over x, z, y_lo).
Axes of the slice: x: 4, y: 4 (y_hi: 2, y_lo: 2; y = y_hi * 2 + y_lo), z: 4, core: 2. Of those that a mesh axis runs over, the one named last changes fastest.
Arguments:
- inputs: bfloat16 [1024, 8192], P(('row', 'col')), may hold values from -6 to 6
- layer_norm_gain: float32 [8192], replicated, may hold values from 0.1 to 1.9
- w_in: bfloat16 [8192, 16384], P('row', 'col'), may hold values from -0.09375 to 0.09375
- w_out: bfloat16 [16384, 8192], P('col', 'row'), may hold values from -0.0625 to 0.0625
- pattern_in: int32 [64, 16], replicated, may hold values from 0 to 31, as said below
- pattern_out: int32 [32, 32], replicated, may hold values from 0 to 63, as said below
- out_grad: bfloat16 [1024, 8192], P(('row', 'col')), may hold values from -6 to 6
Outputs:
- output: bfloat16 [1024, 8192], P(('row', 'col'))
- grad_inputs: bfloat16 [1024, 8192], P(('row', 'col'))
- grad_w_in: bfloat16 [8192, 16384], P('row', 'col')
- grad_w_out: bfloat16 [16384, 8192], P('col', 'row')
- norm_gain_gradient: float32 [8192], replicated
Inputs may be any that keep to these rules, and one draw needn't show every extreme that they name: `pattern_in`: each row lists 8192 / 512 different tile rows in increasing order. `pattern_out`: each row lists 16384 / 512 different tile rows in increasing order.
All inputs are finite; a program needn't handle non-finite values.
Results may differ from a plain program's by a relative error of at most 0.022.
Values may be sent and summed in bfloat16 or wider, within the bound.
A program may use at most 128 MiB of HBM per device.

v0:
```python
import jax
import jax.numpy as jnp
from jax import lax
from jax.sharding import PartitionSpec as P

D = 8192
FF = 16384
BLOCK = 256


def cut_along(shard, dim, count):
    before, after = (shard.shape[:dim], shard.shape[dim + 1 :])
    return jnp.moveaxis(shard.reshape(*before, count, -1, *after), dim, 0)


def sum_at_owner(shard, axis, dim):
    pieces = cut_along(shard, dim, lax.axis_size(axis))
    arrived = lax.all_to_all(pieces, axis, split_axis=0, concat_axis=0, tiled=True)
    return arrived.astype(jnp.float32).sum(axis=0)


def block_mask(pattern, tile_rows):
    iota = jnp.arange(tile_rows, dtype=jnp.int32)
    return jnp.any(pattern[None, :, :] == iota[:, None, None], axis=2)


def apply_mask(weight, mask):
    rows_t, cols_t = mask.shape
    shaped = weight.reshape(rows_t, BLOCK, cols_t, BLOCK)
    kept = jnp.where(mask[:, None, :, None], shaped, jnp.zeros((), weight.dtype))
    return kept.reshape(weight.shape)


def gelu_value(h):
    inner = 0.7978845608 * (h + 0.044715 * h * h * h)
    return 0.5 * h * (1.0 + jnp.tanh(inner))


def gelu_slope(h):
    tanh_v = jnp.tanh(0.7978845608 * (h + 0.044715 * h * h * h))
    return 0.5 * (1.0 + tanh_v) + 0.5 * h * (1.0 - tanh_v * tanh_v) * 0.7978845608 * (
        1.0 + 0.134145 * h * h
    )


def dot_last(left, right):
    return lax.dot_general(
        left, right, (((1,), (1,)), ((), ())), preferred_element_type=jnp.float32
    )


def dot_first(left, right):
    return lax.dot_general(
        left, right, (((0,), (0,)), ((), ())), preferred_element_type=jnp.float32
    )


def shards(inputs, layer_norm_gain, w_in, w_out, pattern_in, pattern_out, out_grad):
    n_row = lax.axis_size("row")
    n_col = lax.axis_size("col")
    row_index = lax.axis_index("row")
    col_index = lax.axis_index("col")
    tok_here = inputs.shape[0]
    feat_tiles = w_in.shape[0] // BLOCK
    unit_tiles = w_in.shape[1] // BLOCK
    mask_in = lax.dynamic_slice(
        block_mask(pattern_in, D // BLOCK),
        (row_index * feat_tiles, col_index * unit_tiles),
        (feat_tiles, unit_tiles),
    )
    mask_out = lax.dynamic_slice(
        block_mask(pattern_out, FF // BLOCK),
        (col_index * unit_tiles, row_index * feat_tiles),
        (unit_tiles, feat_tiles),
    )
    w_in_e = apply_mask(w_in, mask_in)
    w_out_e = apply_mask(w_out, mask_out)
    xfloat = inputs.astype(jnp.float32)
    centered_input = xfloat - jnp.mean(xfloat, axis=1, keepdims=True)
    inverse_deviation = lax.rsqrt(
        jnp.mean(centered_input * centered_input, axis=1, keepdims=True) + 1e-05
    )
    standardized_input = centered_input * inverse_deviation
    normalized_input = (standardized_input * layer_norm_gain[None, :]).astype(jnp.bfloat16)
    swapped = lax.all_to_all(normalized_input, "row", split_axis=1, concat_axis=0, tiled=True)
    allrows = lax.all_gather(swapped, "col", axis=0, tiled=True)
    slice_width = allrows.shape[1]
    byrow = (
        allrows.reshape(n_col, n_row, tok_here, slice_width)
        .transpose(1, 0, 2, 3)
        .reshape(-1, slice_width)
    )
    hidden_pre = lax.psum_scatter(
        jnp.dot(byrow, w_in_e, preferred_element_type=jnp.float32).astype(jnp.bfloat16),
        "row",
        scatter_dimension=0,
        tiled=True,
    ).astype(jnp.float32)
    activation = gelu_value(hidden_pre).astype(jnp.bfloat16)
    w_out_full = lax.all_gather(w_out_e, "row", axis=1, tiled=True)
    summed = sum_at_owner(
        jnp.dot(activation, w_out_full, preferred_element_type=jnp.float32).astype(jnp.bfloat16),
        "col",
        0,
    )
    output = (xfloat + summed).astype(jnp.bfloat16)
    grad_panel = lax.all_gather(out_grad, "col", axis=0, tiled=True)
    d_act = dot_last(grad_panel, w_out_full)
    d_pre = (d_act * gelu_slope(hidden_pre)).astype(jnp.bfloat16)
    w2_sum = lax.psum_scatter(
        dot_first(activation, grad_panel).astype(jnp.bfloat16),
        "row",
        scatter_dimension=1,
        tiled=True,
    )
    grad_w_out = apply_mask(w2_sum, mask_out)
    d_all = lax.all_gather(d_pre, "row", axis=0, tiled=True)
    unit_width = d_all.shape[1]
    panel_terms = jnp.einsum(
        "gtf,gth->gfh",
        byrow.reshape(n_row, -1, slice_width),
        d_all.reshape(n_row, -1, unit_width),
        preferred_element_type=jnp.float32,
    )
    panel_rounded = lax.optimization_barrier(panel_terms.astype(jnp.bfloat16))
    w1_sum = jnp.sum(panel_rounded.astype(jnp.float32), axis=0)
    d_order = (
        d_all.reshape(n_row, n_col, tok_here, unit_width)
        .transpose(1, 0, 2, 3)
        .reshape(-1, unit_width)
    )
    slices = sum_at_owner(dot_last(d_order, w_in_e).astype(jnp.bfloat16), "col", 0)
    normed_gradient = lax.all_to_all(
        slices.astype(jnp.bfloat16), "row", split_axis=0, concat_axis=1, tiled=True
    ).astype(slices.dtype)
    grad_w_in = apply_mask(w1_sum.astype(jnp.bfloat16), mask_in)
    norm_gain_gradient = lax.psum(
        jnp.sum(normed_gradient * standardized_input, axis=0), ("row", "col")
    )
    gain_scaled = normed_gradient * layer_norm_gain[None, :]
    backward_result = inverse_deviation * (
        gain_scaled
        - jnp.mean(gain_scaled, axis=1, keepdims=True)
        - standardized_input * jnp.mean(gain_scaled * standardized_input, axis=1, keepdims=True)
    )
    grad_inputs = (out_grad.astype(jnp.float32) + backward_result).astype(jnp.bfloat16)
    return (output, grad_inputs, grad_w_in, grad_w_out, norm_gain_gradient)


def solution(mesh):
    in_specs = (
        P(("row", "col"), None),
        P(),
        P("row", "col"),
        P("col", "row"),
        P(),
        P(),
        P(("row", "col"), None),
    )
    out_specs = (
        P(("row", "col"), None),
        P(("row", "col"), None),
        P("row", "col"),
        P("col", "row"),
        P(),
    )
    return jax.shard_map(shards, mesh=mesh, in_specs=in_specs, out_specs=out_specs, check_vma=False)
```

profile of v0, /device:TPU:1, one launch (start us, length us, event | category | flops | bytes accessed | tf_op | source)
XLA Modules:
  0.0 768.9 jit_solution(16966023902262134158)
XLA Ops:
  7.2 1.1 convert_reduce_fusion.1
  8.3 1.2 fusion.27
  9.5 1.0 fusion.20
  10.5 10.9 %all_to_all.42 = bf16[8,4,2048]{2,0,1:T(8,128)(2,1)} all-to-all(bf16[8,4,2048]{2,0,1:T(8,128)(2,1)S(1)} %bitcast.58), channel_id=1, replica_groups=mesh['row'=4,'col'=32] {'row'}, dimensions={1} | all-to-all | bytes 262144 | tf_op jit(solution)/shard_map/all_to_all | solution.py:85
  24.2 1.2 copy.32
  25.4 132.9 %all-gather.5.cloned.1.call-done = bf16[1024,2048]{1,0:T(8,128)(2,1)} async-done(((bf16[32,2048]{1,0:T(8,128)(2,1)}), bf16[1024,2048]{1,0:T(8,128)(2,1)}) %all-gather.5.cloned.1.call-update) | async-done | bytes 4194320 | tf_op jit(solution)/shard_map/all_gather | solution.py:86
  158.2 2.6 copy.30
  161.1 3.4 convolution_convert_fusion.4
  164.5 152.4 %all-gather.9.cloned.1.call-done = bf16[256,8192]{1,0:T(8,128)(2,1)} async-done(((bf16[8,8192]{1,0:T(8,128)(2,1)}), bf16[256,8192]{1,0:T(8,128)(2,1)}) %all-gather.9.cloned.1.call-update) | async-done | bytes 4194320 | tf_op jit(solution)/shard_map/all_gather | solution.py:107
  316.9 55.4 %reduce-scatter.3.cloned.1.call-done = bf16[256,512]{1,0:T(8,128)(2,1)} async-done(((bf16[1024,512]{1,0:T(8,128)(2,1)}), bf16[256,512]{1,0:T(8,128)(2,1)}) %reduce-scatter.3.cloned.1.call-update) | async-done | bytes 262160 | tf_op jit(solution)/shard_map/reduce_scatter | solution.py:93
  372.3 8.0 %convolution_convert_fusion = bf16[512,8192]{1,0:T(8,128)(2,1)} fusion(bf16[256,8192]{1,0:T(8,128)(2,1)} %all-gather.9.cloned.1.call-done, bf16[256,512]{1,0:T(8,128)(2,1)} %reduce-scatter.3.cloned.1.call-done), kind=kOutput, calls=%fused_computation | convolution fusion | flops 2152988672 | bytes 12845056 | tf_op jit(solution)/shard_map/dot_general | solution.py:53
  382.5 75.6 %reduce-scatter.5.cloned.1.call-done = bf16[512,2048]{1,0:T(8,128)(2,1)} async-done(((bf16[512,8192]{1,0:T(8,128)(2,1)}), bf16[512,2048]{1,0:T(8,128)(2,1)}) %reduce-scatter.5.cloned.1.call-update) | async-done | bytes 2097168 | tf_op jit(solution)/shard_map/reduce_scatter | solution.py:110
  458.1 4.6 broadcast_select_fusion
  463.0 62.2 %all-gather.7.cloned.1.call-done = bf16[512,8192]{1,0:T(8,128)(2,1)} async-done(((bf16[512,2048]{1,0:T(8,128)(2,1)}), bf16[512,8192]{1,0:T(8,128)(2,1)}) %all-gather.7.cloned.1.call-update) | async-done | bytes 8388624 | tf_op jit(solution)/shard_map/all_gather | solution.py:100
  525.2 7.8 %fusion.3 = bf16[256,512]{1,0:T(8,128)(2,1)} fusion(bf16[512,8192]{1,0:T(8,128)(2,1)} %all-gather.7.cloned.1.call-done, bf16[256,8192]{1,0:T(8,128)(2,1)} %all-gather.9.cloned.1.call-done, bf16[256,512]{1,0:T(8,128)(2,1)S(1)} %copy-done.4), kind=kOutput, calls=%fused_computation.17 | convolution fusion | flops 2150105088 | bytes 13107200 | tf_op jit(solution)/shard_map/dot_general | solution.py:47
  533.1 20.3 %all-gather.11.cloned.1.call-done = bf16[1024,512]{1,0:T(8,128)(2,1)} async-done(((bf16[256,512]{1,0:T(8,128)(2,1)}), bf16[1024,512]{1,0:T(8,128)(2,1)}) %all-gather.11.cloned.1.call-update) | async-done | bytes 1048592 | tf_op jit(solution)/shard_map/all_gather | solution.py:117
  553.4 1.3 copy.35
  554.7 6.0 convolution_convert_fusion.3
  560.7 7.1 all-to-all-start.2
  567.8 7.7 %fusion = bf16[32,8,8192]{2,1,0:T(8,128)(2,1)} fusion(bf16[512,8192]{1,0:T(8,128)(2,1)} %all-gather.7.cloned.1.call-done, bf16[256,512]{1,0:T(8,128)(2,1)S(1)} %copy-done.4), kind=kOutput, calls=%fused_computation.2 | convolution fusion | flops 2150891520 | bytes 12845056 | tf_op jit(solution)/shard_map/dot_general | solution.py:102
  575.5 46.5 %all-to-all-done.2 = bf16[32,32,2048]{2,1,0:T(8,128)(2,1)} async-done(((bf16[32,32,2048]{2,1,0:T(8,128)(2,1)}), bf16[32,32,2048]{2,1,0:T(8,128)(2,1)}, u32[]{:S(2)}, u32[]{:S(2)}) %all-to-all-start.2) | async-done | bytes 4194336 | tf_op jit(solution)/shard_map/all_to_all | solution.py:18
  622.0 10.2 %all-to-all-start.1 = ((bf16[32,8,8192]{2,1,0:T(8,128)(2,1)}), bf16[32,8,8192]{2,1,0:T(8,128)(2,1)}, u32[]{:S(2)}, u32[]{:S(2)}) async-start(bf16[32,8,8192]{2,1,0:T(8,128)(2,1)} %fusion), calls=%async_computation.2 | async-start | bytes 8388608 | tf_op jit(solution)/shard_map/all_to_all | solution.py:18
  632.3 7.8 %convolution_convert_fusion.2 = bf16[4,2048,512]{2,1,0:T(8,128)(2,1)} fusion(bf16[4,256,512]{2,1,0:T(8,128)(2,1)S(1)} %bitcast.53, bf16[4,32,8,2048]{3,2,0,1:T(8,128)(2,1)} %bitcast.45), kind=kOutput, calls=%fused_computation.4 | convolution fusion | flops 2151677952 | bytes 13631488 | tf_op jit(solution)/shard_map/gtf,gth->gfh/dot_general | solution.py:119
  640.1 6.1 reduce_sum.84
  646.2 1.8 broadcast_select_fusion.2
  648.0 3.7 reduce_sum.81
  651.7 33.6 %all-to-all-done.1 = bf16[32,8,8192]{2,1,0:T(8,128)(2,1)} async-done(((bf16[32,8,8192]{2,1,0:T(8,128)(2,1)}), bf16[32,8,8192]{2,1,0:T(8,128)(2,1)}, u32[]{:S(2)}, u32[]{:S(2)}) %all-to-all-start.1) | async-done | bytes 4194336 | tf_op jit(solution)/shard_map/all_to_all | solution.py:18
  685.3 5.7 all-to-all-start.3
  691.0 2.8 convert_reduce_fusion
  693.8 2.3 all-to-all-done.3
  696.6 64.7 %psum.7 = f32[8192]{0:T(1024)} all-reduce(f32[8192]{0:T(1024)S(1)} %get-tuple-element.10), channel_id=1, replica_groups=mesh['row'=4,'col'=32] {'row','col'}, use_global_device_ids=true, to_apply=%region_12.13 | all-reduce | flops 8192 | bytes 65536 | tf_op jit(solution)/shard_map/psum | solution.py:137
  761.3 0.8 fusion.25
  (44 shorter events, 5.9 us)
Async XLA Ops:
  7.2 151.1 %all-gather.5.cloned.1.call-start = ((), (), s32[]{:S(2)}) async-start(), calls=%async_computation.6 | async-start | bytes 4325376 | tf_op jit(solution)/shard_map/all_gather | solution.py:86
  21.4 295.5 %all-gather.9.cloned.1.call-start = ((), (), s32[]{:S(2)}) async-start(), calls=%async_computation.9 | async-start | bytes 4325376 | tf_op jit(solution)/shard_map/all_gather | solution.py:107
  22.2 350.1 %reduce-scatter.3.cloned.1.call-start = ((), (), s32[]{:S(2)}) async-start(), calls=%async_computation.7 | async-start | bytes 1310720 | tf_op jit(solution)/shard_map/reduce_scatter | solution.py:93
  158.2 2.9 copy-start.6
  164.5 293.6 %reduce-scatter.5.cloned.1.call-start = ((), (), s32[]{:S(2)}) async-start(), calls=%async_computation.11 | async-start | bytes 10485760 | tf_op jit(solution)/shard_map/reduce_scatter | solution.py:110
  380.4 0.7 copy-start.5
  380.4 144.8 %all-gather.7.cloned.1.call-start = ((), (), s32[]{:S(2)}) async-start(), calls=%async_computation.8 | async-start | bytes 10485760 | tf_op jit(solution)/shard_map/all_gather | solution.py:100
  458.1 67.1 %copy-start.4 = (bf16[256,512]{1,0:T(8,128)(2,1)S(1)}, bf16[256,512]{1,0:T(8,128)(2,1)}, u32[]{:S(2)}) copy-start(bf16[256,512]{1,0:T(8,128)(2,1)} %reduce-scatter.3.cloned.1.call-done) | copy-start | bytes 786436
  462.8 90.6 %all-gather.11.cloned.1.call-start = ((), (), s32[]{:S(2)}) async-start(), calls=%async_computation.10 | async-start | bytes 1310720 | tf_op jit(solution)/shard_map/all_gather | solution.py:117
  560.7 61.4 %all-to-all-start.2 = ((bf16[32,32,2048]{2,1,0:T(8,128)(2,1)}), bf16[32,32,2048]{2,1,0:T(8,128)(2,1)}, u32[]{:S(2)}, u32[]{:S(2)}) async-start(bf16[32,32,2048]{2,1,0:T(8,128)(2,1)} %bitcast.47), calls=%async_computation.3 | async-start | bytes 8388608 | tf_op jit(solution)/shard_map/all_to_all | solution.py:18
  575.5 56.7 %copy-start.2 = (f32[8192]{0:T(1024)S(1)}, f32[8192]{0:T(1024)}, u32[]{:S(2)}) copy-start(f32[8192]{0:T(1024)} %param.8) | copy-start | bytes 98308
  575.5 56.7 %copy-start = (bf16[1024,512]{1,0:T(8,128)(2,1)S(1)}, bf16[1024,512]{1,0:T(8,128)(2,1)}, u32[]{:S(2)}) copy-start(bf16[1024,512]{1,0:T(8,128)(2,1)} %all-gather.11.cloned.1.call-done) | copy-start | bytes 3145732
  622.0 63.3 %all-to-all-start.1 = ((bf16[32,8,8192]{2,1,0:T(8,128)(2,1)}), bf16[32,8,8192]{2,1,0:T(8,128)(2,1)}, u32[]{:S(2)}, u32[]{:S(2)}) async-start(bf16[32,8,8192]{2,1,0:T(8,128)(2,1)} %fusion), calls=%async_computation.2 | async-start | bytes 8388608 | tf_op jit(solution)/shard_map/all_to_all | solution.py:18
  648.0 48.3 %copy-start.1 = (bf16[8,8192]{1,0:T(8,128)(2,1)S(1)}, bf16[8,8192]{1,0:T(8,128)(2,1)}, u32[]{:S(2)}) copy-start(bf16[8,8192]{1,0:T(8,128)(2,1)} %param.7) | copy-start | bytes 393220
  648.0 113.3 %copy-start.3 = (bf16[8,8192]{1,0:T(8,128)(2,1)S(1)}, bf16[8,8192]{1,0:T(8,128)(2,1)}, u32[]{:S(2)}) copy-start(bf16[8,8192]{1,0:T(8,128)(2,1)} %param.13) | copy-start | bytes 393220
  685.3 10.8 %all-to-all-start.3 = ((bf16[4,8,2048]{2,1,0:T(8,128)(2,1)}), bf16[4,8,2048]{2,1,0:T(8,128)(2,1)S(1)}, u32[]{:S(2)}, u32[]{:S(2)}) async-start(bf16[4,8,2048]{2,1,0:T(8,128)(2,1)} %bitcast.12), calls=%async_computation.4 | async-start | bytes 262144 | tf_op jit(solution)/shard_map/all_to_all | solution.py:133
Sparse Core Ops, SparseCore 0:
  21.6 136.6 all-gather.4
  159.9 157.0 all-gather.8
  320.1 52.1 reduce-scatter.2
  380.5 77.5 reduce-scatter.4
  462.9 62.2 all-gather.6
  533.2 20.1 all-gather.10
where the time goes:
time: 770 us; the launch traced here: 769 us
  waiting for transfers between devices  582 us (76%)
  blocking collectives  75.6 us (10%)
  matrix products  40.8 us (5%)
  other arithmetic  24.6 us (3%)
  starting transfers between devices  23.4 us (3%)
  between operations  14.2 us (2%)
  local copies, waits for them, and re-layouts  8.34 us (1%)
    all_gather x1, waiting for transfers between devices, shards(): grad_panel = lax.all_gather(out_grad, 'col', axis=0, tiled=True)  152 us
    all_gather x1, waiting for transfers between devices, shards(): allrows = lax.all_gather(swapped, 'col', axis=0, tiled=True)  133 us
    all_to_all x2, waiting for transfers between devices, sum_at_owner(): lax.all_to_all(pieces, axis, split_axis=0, concat_axis=0, tiled=True)  80.1 us
    reduce_scatter x1, waiting for transfers between devices, shards(): lax.psum_scatter(dot_first(activation, grad_panel).astype(jnp.bfloat16),...  75.6 us
    psum x1, blocking collectives, shards(): lax.psum(jnp.sum(normed_gradient * standardized_input, axis=0), ('row', '...  64.7 us
    all_gather x1, waiting for transfers between devices, shards(): w_out_full = lax.all_gather(w_out_e, 'row', axis=1, tiled=True)  62.2 us
    reduce_scatter x1, waiting for transfers between devices, shards(): lax.psum_scatter(jnp.dot(byrow, w_in_e, preferred_element_type=jnp.float3...  55.4 us
    all_gather x1, waiting for transfers between devices, shards(): d_all = lax.all_gather(d_pre, 'row', axis=0, tiled=True)  20.3 us
  transfers between devices with their start and end apart: 9, of which 9 were waited for; matrix products, arithmetic and copies ran while one was open for 5% of the time, Pallas kernels for 0%

commit v1 on v0

v1 whole, which is shorter than its diff:
```python
import functools

import jax
import jax.numpy as jnp
from jax import lax
from jax.experimental import pallas as pl
from jax.experimental.pallas import tpu as pltpu
from jax.sharding import PartitionSpec as P

BLOCK = 256
BF = jnp.bfloat16
F32 = jnp.float32
N_COPIES = 192


def gelu_value(h):
    inner = 0.7978845608 * (h + 0.044715 * h * h * h)
    return 0.5 * h * (1.0 + jnp.tanh(inner))


def gelu_slope(h):
    tanh_v = jnp.tanh(0.7978845608 * (h + 0.044715 * h * h * h))
    return 0.5 * (1.0 + tanh_v) + 0.5 * h * (1.0 - tanh_v * tanh_v) * 0.7978845608 * (
        1.0 + 0.134145 * h * h
    )


def dot_nn(a, b):
    return lax.dot_general(a, b, (((1,), (0,)), ((), ())), preferred_element_type=F32)


def dot_nt(a, b):
    return lax.dot_general(a, b, (((1,), (1,)), ((), ())), preferred_element_type=F32)


def dot_tn(a, b):
    return lax.dot_general(a, b, (((0,), (0,)), ((), ())), preferred_element_type=F32)


def kernel(
    x_ref, gain_ref, gain64_ref, og_ref, win_hbm, wout_hbm, min_ref, mout_ref,
    out_ref, gin_ref, gwin_ref, gwout_ref, gg_ref,
    win, wout, normed, s0x, s0g, gx, gg,
    ar_send, ar_recv, ay_send, ay_recv, acc, act, dpre,
    rs_far, rs_half, rs_full, rs_in, rs_own,
    ru_far, ru_half, ru_full, ru_in,
    rfin, e_buf, gw1, gw2, s_x, s_z, s_c,
    send_sem, recv_sem, w_sem,
):
    row = lax.axis_index("row")
    col = lax.axis_index("col")
    xi, zi, yl = col // 8, (col // 2) % 4, col % 2
    yh, core = row // 2, row % 2
    q = row * 2 + yl

    def dev(x, z, qq):
        return (qq // 2, (x * 4 + z) * 2 + qq % 2)

    used = [0]

    def copy(src, dst, to):
        i = used[0]
        used[0] += 1
        c = pltpu.make_async_remote_copy(
            src_ref=src, dst_ref=dst, send_sem=send_sem.at[i], recv_sem=recv_sem.at[i],
            device_id=to, device_id_type=pl.DeviceIdType.MESH,
        )
        sent.append(c)
        return c

    sent = []

    def go(src, dst, to):
        c = copy(src, dst, to)
        c.start()
        return c

    def step(i, n):
        return (i + n + 4) % 4

    sibling = (yh * 2 + (1 - core), col)
    partner = ((1 - yh) * 2 + core, col)

    w_in_copy = pltpu.make_async_copy(win_hbm, win, w_sem.at[0])
    w_out_copy = pltpu.make_async_copy(wout_hbm, wout, w_sem.at[1])
    w_in_copy.start()
    w_out_copy.start()

    barrier = pltpu.get_barrier_semaphore()
    peers = [dev(step(xi, n), zi, q) for n in (1, 2, 3)]
    peers += [dev(xi, step(zi, n), q) for n in (1, 2, 3)]
    peers += [dev(xi, zi, (q + n) % 8) for n in range(1, 8)]
    for p in peers:
        pl.semaphore_signal(barrier, inc=1, device_id=p, device_id_type=pl.DeviceIdType.MESH)

    xf = x_ref[...].astype(F32)
    cen = xf - jnp.mean(xf, axis=1, keepdims=True)
    inv = lax.rsqrt(jnp.mean(cen * cen, axis=1, keepdims=True) + 1e-05)
    nrm = (cen * inv * gain_ref[...]).astype(BF)
    for r in range(4):
        normed[r] = nrm[:, r * 2048 : (r + 1) * 2048]
    pl.semaphore_wait(barrier, len(peers))

    def column_in(src_of, dst):
        cs = []
        for n in range(1, 8):
            qq = (q + n) % 8
            cs.append(go(src_of(qq), dst.at[q], dev(xi, zi, qq)))
        return cs

    c0x = column_in(lambda qq: normed.at[qq // 2], s0x)
    c0g = column_in(
        lambda qq: og_ref.at[:, pl.ds(pl.multiple_of((qq // 2) * 2048, 2048), 2048)], s0g
    )
    s0x[q] = normed[row]
    s0g[q] = og_ref[:, pl.ds(pl.multiple_of(row * 2048, 2048), 2048)]

    w_in_copy.wait()
    for t in range(8):
        win[t * 256 : (t + 1) * 256] = win[t * 256 : (t + 1) * 256] * min_ref[t : t + 1].astype(BF)
    w_out_copy.wait()
    for t in range(2):
        wout[t * 256 : (t + 1) * 256] = wout[t * 256 : (t + 1) * 256] * mout_ref[t : t + 1].astype(BF)

    def blk(g, k, u, v):
        return g.at[0, v, u] if k == 0 else g.at[1, u, v]

    def gather(s0, g, arrived):
        for c in arrived:
            c.wait_recv()
        block = s0[...].reshape(64, 2048)
        g[0, xi, zi] = block[:, :1024]
        g[1, xi, zi] = block[:, 1024:]
        st = []
        for k in range(2):
            u0, v0 = (zi, xi) if k == 0 else (xi, zi)

            def to_u(n, k=k):
                return dev(xi, step(zi, n), q) if k == 0 else dev(step(xi, n), zi, q)

            def to_v(n, k=k):
                return dev(step(xi, n), zi, q) if k == 0 else dev(xi, step(zi, n), q)

            st.append(dict(k=k, u0=u0, v0=v0, to_u=to_u, to_v=to_v))

        def both(s, u, v, to):
            b = blk(g, s["k"], u, v)
            return {n: go(b, b, to(n)) for n in (1, -1)}

        for s in st:
            s["f"] = both(s, s["u0"], s["v0"], s["to_u"])
            s["s"] = {0: both(s, s["u0"], s["v0"], s["to_v"])}
            s["f2"], s["s2"] = {}, []
        yield
        for n in (1, -1):
            for s in st:
                s["f"][n].wait_recv()
                u = step(s["u0"], -n)
                b = blk(g, s["k"], u, s["v0"])
                part = b.at[pl.ds(0, 32)] if n == 1 else b.at[pl.ds(32, 32)]
                s["f2"][n] = go(part, part, s["to_u"](n))
                s["s"][-n] = both(s, u, s["v0"], s["to_v"])
            yield
        for n in (1, -1):
            for s in st:
                s["s"][0][n].wait_recv()
                if n == 1:
                    b = blk(g, s["k"], s["u0"], step(s["v0"], -n))
                    s["s2"].append(go(b, b, s["to_v"](n)))
        for s in st:
            s["f2"][1].wait_recv()
            s["f2"][-1].wait_recv()
            s["s"][2] = both(s, step(s["u0"], 2), s["v0"], s["to_v"])
        yield
        for off in (-1, 1):
            for n in (1, -1):
                for s in st:
                    s["s"][off][n].wait_recv()
                    if n == off:
                        b = blk(g, s["k"], step(s["u0"], off), step(s["v0"], -n))
                        s["s2"].append(go(b, b, s["to_v"](n)))
            yield
        for n in (1, -1):
            for s in st:
                s["s"][2][n].wait_recv()
                if n == -1:
                    b = blk(g, s["k"], step(s["u0"], 2), step(s["v0"], -n))
                    s["s2"].append(go(b, b, s["to_v"](n)))
        yield
        for s in st:
            for c in s["s2"]:
                c.wait_recv()

    def drain(g, n=None):
        for i, _ in enumerate(g):
            if n is not None and i + 1 >= n:
                return

    gen_x = gather(s0x, gx, c0x)
    gen_g = gather(s0g, gg, c0g)
    drain(gen_x, 1)
    drain(gen_g, 1)
    for _ in range(3):
        drain(gen_x, 1)
        drain(gen_g, 1)
    drain(gen_x)

    def partial(g, w, nt, xx):
        a = g[0, xx].reshape(256, 1024)
        b = g[1, xx].reshape(256, 1024)
        if nt:
            return dot_nt(a, w[:, :1024]) + dot_nt(b, w[:, 1024:])
        return dot_nn(a, w[:1024]) + dot_nn(b, w[1024:])

    def row_sum_a(i, g, w, nt):
        def other(j, _):
            ar_send[i, j] = partial(g, w, nt, 2 * (1 - core) + j).astype(BF)
            return 0

        lax.fori_loop(0, 2, other, 0)
        return go(ar_send.at[i], ar_recv.at[i], sibling)

    def row_sum_b(i, g, w, nt, c):
        def mine(j, _):
            acc[i, j] = partial(g, w, nt, 2 * core + j)
            return 0

        lax.fori_loop(0, 2, mine, 0)
        c.wait_recv()

        def add(j, _):
            v = acc[i, j] + ar_recv[i, j].astype(F32)
            acc[i, j] = v
            ay_send[i, j] = v.astype(BF)
            return 0

        lax.fori_loop(0, 2, add, 0)
        return go(ay_send.at[i], ay_recv.at[i], partner)

    def rows_loop(f):
        def body(j, _):
            h, m = j // 4, j % 4
            f(h, m, pl.ds(pl.multiple_of(m * 64, 64), 64))
            return 0

        lax.fori_loop(0, 8, body, 0)

    ca = row_sum_a(0, gx, win, False)
    drain(gen_g, 1)
    cb = row_sum_b(0, gx, win, False, ca)
    drain(gen_g)
    ca1 = row_sum_a(1, gg, wout, True)
    cb.wait_recv()

    def act_rows(h, m, rows):
        pre = acc[0, h, rows] + ay_recv[0, h, rows].astype(F32)
        acc[0, h, rows] = pre
        act[2 * core + h, m] = gelu_value(pre).astype(BF)

    rows_loop(act_rows)
    mine2 = pl.ds(2 * core, 2)
    cc = go(act.at[mine2], act.at[mine2], sibling)
    cb1 = row_sum_b(1, gg, wout, True, ca1)

    def term(t, k, v):
        if t == 0:
            a = act[v] if k == 0 else act[:, v]
            return dot_nn(a.reshape(256, 512), wout[:, k * 1024 : (k + 1) * 1024])
        a = dpre[v] if k == 0 else dpre[:, v]
        return dot_nt(a.reshape(256, 512), win[k * 1024 : (k + 1) * 1024, :])

    def scatter(t):
        st = []
        for k in range(2):
            u0, v0 = (zi, xi) if k == 0 else (xi, zi)

            def to_u(n, k=k):
                return dev(xi, step(zi, n), q) if k == 0 else dev(step(xi, n), zi, q)

            def to_v(n, k=k):
                return dev(step(xi, n), zi, q) if k == 0 else dev(xi, step(zi, n), q)

            st.append(dict(k=k, u0=u0, v0=v0, to_u=to_u, to_v=to_v))
        for s in st:
            k = s["k"]
            rs_far[t, k] = term(t, k, step(s["v0"], 2)).astype(BF).reshape(4, 64, 1024)
            s["h"] = {
                n: go(
                    rs_far.at[t, k, pl.ds(0 if n == 1 else 2, 2)],
                    rs_half.at[t, k, 0 if n == 1 else 1],
                    s["to_v"](n),
                )
                for n in (1, -1)
            }
        yield
        for n in (1, -1):
            for s in st:
                k = s["k"]
                j = 0 if n == 1 else 1
                p = term(t, k, step(s["v0"], n)).reshape(4, 64, 1024)
                s["h"][n].wait_recv()
                lo, hi = p[0:2], p[2:4]
                extra = rs_half[t, k, j].astype(F32)
                if n == 1:
                    lo = lo + extra
                else:
                    hi = hi + extra
                rs_full[t, k, j, 0:2] = lo.astype(BF)
                rs_full[t, k, j, 2:4] = hi.astype(BF)
                s.setdefault("w", {})[n] = go(
                    rs_full.at[t, k, j], rs_in.at[t, k, j], s["to_v"](n)
                )
            yield
        for s in st:
            k = s["k"]
            rs_own[k] = term(t, k, s["v0"]).reshape(4, 64, 1024)
        yield
        for s in st:
            k = s["k"]
            s["w"][1].wait_recv()
            s["w"][-1].wait_recv()

            def summed(u, k=k):
                return (
                    rs_own[k, u]
                    + rs_in[t, k, 0, u].astype(F32)
                    + rs_in[t, k, 1, u].astype(F32)
                )

            s["sum"] = summed
            ru_far[t, k] = summed(step(s["u0"], 2)).astype(BF)
            s["uh"] = {
                n: go(
                    ru_far.at[t, k, pl.ds(0 if n == 1 else 32, 32)],
                    ru_half.at[t, k, 0 if n == 1 else 1],
                    s["to_u"](n),
                )
                for n in (1, -1)
            }
        yield
        for n in (1, -1):
            for s in st:
                k = s["k"]
                j = 0 if n == 1 else 1
                p = s["sum"](step(s["u0"], n))
                s["uh"][n].wait_recv()
                extra = ru_half[t, k, j].astype(F32)
                lo, hi = p[0:32], p[32:64]
                if n == 1:
                    lo = lo + extra
                else:
                    hi = hi + extra
                ru_full[t, k, j, 0:32] = lo.astype(BF)
                ru_full[t, k, j, 32:64] = hi.astype(BF)
                s.setdefault("uw", {})[n] = go(
                    ru_full.at[t, k, j], ru_in.at[t, k, j], s["to_u"](n)
                )
        yield
        for s in st:
            k = s["k"]
            s["uw"][1].wait_recv()
            s["uw"][-1].wait_recv()
            r = s["sum"](s["u0"]) + ru_in[t, k, 0].astype(F32) + ru_in[t, k, 1].astype(F32)
            rfin[t, :, :, k * 1024 : (k + 1) * 1024] = r.astype(BF).reshape(8, 8, 1024)
        cs = []
        for n in range(1, 8):
            qq = (q + n) % 8
            cs.append(go(rfin.at[t, qq], e_buf.at[t, q], dev(xi, zi, qq)))
        e_buf[t, q] = rfin[t, q]
        last[t] = cs

    last = {}
    cc.wait_recv()
    gen_o = scatter(0)
    drain(gen_o, 1)
    drain(gen_o, 2)
    cb1.wait_recv()

    def dpre_rows(h, m, rows):
        d = acc[1, h, rows] + ay_recv[1, h, rows].astype(F32)
        dpre[2 * core + h, m] = (d * gelu_slope(acc[0, h, rows])).astype(BF)

    rows_loop(dpre_rows)
    cd = go(dpre.at[mine2], dpre.at[mine2], sibling)
    drain(gen_o, 1)
    cd.wait_recv()
    drain(gen_o)
    gen_d = scatter(1)
    drain(gen_d, 1)
    drain(gen_d, 2)

    ones = jnp.ones((8, 512), BF)
    for k in range(2):

        def win_tile(j, _, k=k):
            lanes = pl.ds(pl.multiple_of(j * 256, 256), 256)
            ft = k * 4 + j
            a = gx[k, :, :, :, lanes].reshape(1024, 256)
            raw = dot_tn(a, dpre[...].reshape(1024, 512))
            rows = pl.ds(pl.multiple_of(ft * 256, 256), 256)
            gw1[rows] = (raw * min_ref[pl.ds(ft, 1)]).astype(BF)
            p = raw * win[rows].astype(F32)
            hi = p.astype(BF)
            lo = (p - hi.astype(F32)).astype(BF)
            s = dot_nt(ones, hi) + dot_nt(ones, lo)
            s_x[xi, pl.ds(2 * ft, 1)] = s[0:1, :128]
            s_x[xi, pl.ds(2 * ft + 1, 1)] = s[0:1, 128:]
            return 0

        lax.fori_loop(0, 4, win_tile, 0)
    o1 = pltpu.make_async_copy(gw1, gwin_ref, w_sem.at[0])
    o1.start()
    sx = [go(s_x.at[xi], s_x.at[xi], dev(step(xi, n), zi, q)) for n in (1, 2, 3)]
    drain(gen_d, 1)
    for k in range(2):

        def wout_tile(j, _, k=k):
            lanes = pl.ds(pl.multiple_of(j * 256, 256), 256)
            b = gg[k, :, :, :, lanes].reshape(1024, 256)
            raw = dot_tn(act[...].reshape(1024, 512), b)
            cols = pl.ds(pl.multiple_of(k * 1024 + j * 256, 256), 256)
            for h in range(2):
                gw2[h * 256 : (h + 1) * 256, cols] = (
                    raw[h * 256 : (h + 1) * 256] * mout_ref[h : h + 1, cols]
                ).astype(BF)
            return 0

        lax.fori_loop(0, 4, wout_tile, 0)
    o2 = pltpu.make_async_copy(gw2, gwout_ref, w_sem.at[1])
    o2.start()
    for c in sx:
        c.wait_recv()
    s_z[zi] = (s_x[0] + s_x[1]) + (s_x[2] + s_x[3])
    sz = [go(s_z.at[zi], s_z.at[zi], dev(xi, step(zi, n), q)) for n in (1, 2, 3)]
    drain(gen_d, 1)
    for c in sz:
        c.wait_recv()
    s_c[q] = (s_z[0] + s_z[1]) + (s_z[2] + s_z[3])
    sc = [go(s_c.at[q], s_c.at[q], dev(xi, zi, (q + n) % 8)) for n in range(1, 8)]
    drain(gen_d)

    for c in last[0]:
        c.wait_recv()
    for r in range(4):
        f = slice(r * 2048, (r + 1) * 2048)
        o = e_buf[0, 2 * r].astype(F32) + e_buf[0, 2 * r + 1].astype(F32)
        out_ref[:, f] = (x_ref[:, f].astype(F32) + o).astype(BF)
    for c in sc:
        c.wait_recv()
    for r in range(4):
        gg_ref[r * 16 : (r + 1) * 16] = (s_c[2 * r] + s_c[2 * r + 1]) / gain64_ref[r * 16 : (r + 1) * 16]

    for c in last[1]:
        c.wait_recv()
    parts = [
        e_buf[1, 2 * r].astype(F32) + e_buf[1, 2 * r + 1].astype(F32) for r in range(4)
    ]
    d = jnp.concatenate(parts, axis=1)
    xf = x_ref[...].astype(F32)
    cen = xf - jnp.mean(xf, axis=1, keepdims=True)
    inv = lax.rsqrt(jnp.mean(cen * cen, axis=1, keepdims=True) + 1e-05)
    hat = cen * inv
    g = d * gain_ref[...]
    back = inv * (
        g - jnp.mean(g, axis=1, keepdims=True) - hat * jnp.mean(g * hat, axis=1, keepdims=True)
    )
    gin_ref[...] = (og_ref[...].astype(F32) + back).astype(BF)
    for c in sent:
        c.wait_send()
    o1.wait()
    o2.wait()


def tile_mask(pattern, tile_rows):
    iota = jnp.arange(tile_rows, dtype=jnp.int32)
    return jnp.any(pattern[None, :, :] == iota[:, None, None], axis=2)


def shards(inputs, layer_norm_gain, w_in, w_out, pattern_in, pattern_out, out_grad):
    row = lax.axis_index("row")
    col = lax.axis_index("col")
    m_in = lax.dynamic_slice(tile_mask(pattern_in, 32), (row * 8, col * 2), (8, 2))
    m_out = lax.dynamic_slice(tile_mask(pattern_out, 64), (col * 2, row * 8), (2, 8))
    m_in = jnp.repeat(m_in.astype(F32), BLOCK, axis=1)
    m_out = jnp.repeat(m_out.astype(F32), BLOCK, axis=1)
    vm = functools.partial(pl.BlockSpec, memory_space=pltpu.VMEM)
    hbm = functools.partial(pl.BlockSpec, memory_space=pl.ANY)
    V = pltpu.VMEM
    out = pl.pallas_call(
        kernel,
        out_shape=(
            jax.ShapeDtypeStruct((8, 8192), BF),
            jax.ShapeDtypeStruct((8, 8192), BF),
            jax.ShapeDtypeStruct((2048, 512), BF),
            jax.ShapeDtypeStruct((512, 2048), BF),
            jax.ShapeDtypeStruct((64, 128), F32),
        ),
        in_specs=[vm(), vm(), vm(), vm(), hbm(), hbm(), vm(), vm()],
        out_specs=(vm(), vm(), hbm(), hbm(), vm()),
        scratch_shapes=[
            V((2048, 512), BF),
            V((512, 2048), BF),
            V((4, 8, 2048), BF),
            V((8, 8, 2048), BF),
            V((8, 8, 2048), BF),
            V((2, 4, 4, 64, 1024), BF),
            V((2, 4, 4, 64, 1024), BF),
            V((2, 2, 256, 512), BF),
            V((2, 2, 256, 512), BF),
            V((2, 2, 256, 512), BF),
            V((2, 2, 256, 512), BF),
            V((2, 2, 256, 512), F32),
            V((4, 4, 64, 512), BF),
            V((4, 4, 64, 512), BF),
            V((2, 2, 4, 64, 1024), BF),
            V((2, 2, 2, 2, 64, 1024), BF),
            V((2, 2, 2, 4, 64, 1024), BF),
            V((2, 2, 2, 4, 64, 1024), BF),
            V((2, 4, 64, 1024), F32),
            V((2, 2, 64, 1024), BF),
            V((2, 2, 2, 32, 1024), BF),
            V((2, 2, 2, 64, 1024), BF),
            V((2, 2, 2, 64, 1024), BF),
            V((2, 8, 8, 2048), BF),
            V((2, 8, 8, 2048), BF),
            V((2048, 512), BF),
            V((512, 2048), BF),
            V((4, 16, 128), F32),
            V((4, 16, 128), F32),
            V((8, 16, 128), F32),
            pltpu.SemaphoreType.DMA((N_COPIES,)),
            pltpu.SemaphoreType.DMA((N_COPIES,)),
            pltpu.SemaphoreType.DMA((2,)),
        ],
        compiler_params=pltpu.CompilerParams(
            collective_id=0, has_side_effects=True, vmem_limit_bytes=67_043_328
        ),
        name="ffn",
    )(
        inputs, layer_norm_gain.reshape(1, 8192), layer_norm_gain.reshape(64, 128), out_grad,
        w_in, w_out, m_in, m_out,
    )
    output, grad_inputs, g_in, g_out, g_gain = out
    return output, grad_inputs, g_in, g_out, g_gain.reshape(8192)


def solution(mesh):
    in_specs = (
        P(("row", "col"), None),
        P(),
        P("row", "col"),
        P("col", "row"),
        P(),
        P(),
        P(("row", "col"), None),
    )
    out_specs = (
        P(("row", "col"), None),
        P(("row", "col"), None),
        P("row", "col"),
        P("col", "row"),
        P(),
    )
    return jax.shard_map(shards, mesh=mesh, in_specs=in_specs, out_specs=out_specs, check_vma=False)
```

time: 770 us -> 160 us (0.21)
  waiting for transfers between devices: 582 us -> 0 us
  Pallas kernels: 0 us -> 147 us
  blocking collectives: 75.6 us -> 0 us
  matrix products: 40.8 us -> 0 us
  starting transfers between devices: 23.4 us -> 0 us
  other arithmetic: 24.6 us -> 1.88 us
  between operations: 14.2 us -> 0.66 us
    all_gather x4 -> x0, waiting for transfers between devices: 368 us -> none  [the longest x1 152 us: shards(): grad_panel = lax.all_gather(out_grad, 'col', axis=0, tiled=True)]
    pallas_call x0 -> x1, Pallas kernels: none -> 147 us  [shards(): pl.pallas_call(kernel, out_shape=(jax.ShapeDtypeStruct((8, 8192), BF), ja...]
    reduce_scatter x2 -> x0, waiting for transfers between devices: 131 us -> none  [the longest x1 75.6 us: shards(): lax.psum_scatter(dot_first(activation, grad_panel).astype(jnp.bfloat16),...]
    all_to_all x3 -> x0, waiting for transfers between devices: 82.4 us -> none  [the longest x2 80.1 us: sum_at_owner(): lax.all_to_all(pieces, axis, split_axis=0, concat_axis=0, tiled=True)]
    psum x1 -> x0, blocking collectives: 64.7 us -> none  [shards(): lax.psum(jnp.sum(normed_gradient * standardized_input, axis=0), ('row', '...]
    dot_general x6 -> x0, matrix products: 40.8 us -> none  [the longest x2 13.8 us: dot_last(): lax.dot_general(left, right, (((1,), (1,)), ((), ())), preferred_element_...]
    all_to_all x3 -> x0, starting transfers between devices: 23 us -> none  [the longest x2 17.3 us: sum_at_owner(): lax.all_to_all(pieces, axis, split_axis=0, concat_axis=0, tiled=True)]
    reduce_sum x7 -> x0, other arithmetic: 15.3 us -> none  [the longest x2 6.48 us: sum_at_owner(): return arrived.astype(jnp.float32).sum(axis=0)]
  transfers between devices with their start and end apart: 9 -> 0, of which waited for: 9 -> 0; matrix products, arithmetic and copies ran while one was open for 5% -> 0% of each run, Pallas kernels for 0% -> 0%
where the time goes in v1:
time: 160 us; the launch traced here: 159 us
  Pallas kernels  147 us (92%)
  local copies, waits for them, and re-layouts  9.81 us (6%)
  other arithmetic  1.88 us (1%)
    pallas_call x1, Pallas kernels, shards(): pl.pallas_call(kernel, out_shape=(jax.ShapeDtypeStruct((8, 8192), BF), ja...  147 us
    unnamed x11, local copies, waits for them, and re-layouts  8.96 us

profile of v1, /device:TPU:1, one launch (start us, length us, event | category | flops | bytes accessed | tf_op | source)
XLA Modules:
  0.0 159.3 jit_solution(4276396545846665408)
XLA Ops:
  0.6 0.8 fusion.1
  1.4 0.1 dynamic-slice_convert_fusion.1
  1.5 0.1 copy.13
  1.6 0.9 fusion
  2.5 0.1 dynamic-slice_convert_fusion
  2.6 0.1 copy.14
  2.7 0.1 broadcast_bitcast_fusion
  2.8 0.6 copy.15
  3.4 0.7 broadcast_in_dim.4
  4.1 147.0 %ffn.1 = (bf16[8,8192]{1,0:T(8,128)(2,1)}, bf16[8,8192]{1,0:T(8,128)(2,1)}, bf16[2048,512]{1,0:T(8,128)(2,1)}, bf16[512,2048]{1,0:T(8,128)(2,1)}, f32[64,128]{1,0:T(8,128)}) custom-call(bf16[8,8192]{1,0:T(8,128)(2,1)} %x_ref.1, f32[1,8192]{1,0:T(1,128)} %bitcast.7, f32[64,128]{1,0:T(8,128)} %bitcast.8, bf16[8,8192]{1,0:T(8,128)(2,1)} %og_ref.1, ...), custom_call_target="tpu_custom_call" | custom-call | tf_op jit(solution)/shard_map/ffn/pallas_call | solution.py:489
  151.1 1.6 copy.21
  152.6 1.6 copy.22
  154.2 0.0 copy-start
  154.2 3.2 %copy.23 = bf16[2048,512]{1,0:T(8,128)(2,1)} copy(bf16[2048,512]{1,0:T(8,128)(2,1)} %get-tuple-element.22) | data formatting | bytes 4194304
  157.4 0.0 copy-done
  157.4 0.0 copy-start.1
  157.4 1.3 copy.24
  158.7 0.0 copy-done.1
  158.7 0.6 copy.25
Async XLA Ops:
  154.2 3.2 %copy-start = (bf16[512,2048]{1,0:T(8,128)(2,1)S(1)}, bf16[512,2048]{1,0:T(8,128)(2,1)}, u32[]{:S(2)}) copy-start(bf16[512,2048]{1,0:T(8,128)(2,1)} %get-tuple-element.23) | copy-start | bytes 6291460
  157.4 1.3 copy-start.1

commit v2 on v1

v2 whole, which is shorter than its diff:
```python
import functools

import jax
import jax.numpy as jnp
from jax import lax
from jax.experimental import pallas as pl
from jax.experimental.pallas import tpu as pltpu
from jax.sharding import PartitionSpec as P

BF = jnp.bfloat16
F32 = jnp.float32
N_COPIES = 256


def gelu_value(h):
    inner = 0.7978845608 * (h + 0.044715 * h * h * h)
    return 0.5 * h * (1.0 + jnp.tanh(inner))


def gelu_slope(h):
    tanh_v = jnp.tanh(0.7978845608 * (h + 0.044715 * h * h * h))
    return 0.5 * (1.0 + tanh_v) + 0.5 * h * (1.0 - tanh_v * tanh_v) * 0.7978845608 * (
        1.0 + 0.134145 * h * h
    )


def dot_nn(a, b):
    return lax.dot_general(a, b, (((1,), (0,)), ((), ())), preferred_element_type=F32)


def dot_nt(a, b):
    return lax.dot_general(a, b, (((1,), (1,)), ((), ())), preferred_element_type=F32)


def dot_tn(a, b):
    return lax.dot_general(a, b, (((0,), (0,)), ((), ())), preferred_element_type=F32)


class Sent:
    def __init__(self, c):
        self.c, self.got = c, False
        c.start()

    def wait_recv(self):
        self.got = True
        self.c.wait_recv()


def kernel(
    x_ref, gain_ref, gain64_ref, og_ref, win_hbm, wout_hbm, pin_ref, pout_ref,
    out_ref, gin_ref, gwin_ref, gwout_ref, gg_ref,
    win, wout, min_ref, mout_ref, normed, s0x, s0g, gx, gg,
    ar_send, ar_recv, ay_send, ay_recv, acc, act, dpre,
    rs_far, rs_half, rs_full, rs_in, rs_p,
    ru_far, ru_half, ru_full, ru_in,
    rfin, e_buf, gw1, gw2, s_x, s_z, s_c,
    send_sem, recv_sem, w_sem,
):
    row = lax.axis_index("row")
    col = lax.axis_index("col")
    xi, zi, yl = col // 8, (col // 2) % 4, col % 2
    yh, core = row // 2, row % 2
    q = row * 2 + yl

    def dev(x, z, qq):
        return (qq // 2, (x * 4 + z) * 2 + qq % 2)

    sent = []
    outs = []

    def go(src, dst, to):
        i = len(sent)
        c = Sent(
            pltpu.make_async_remote_copy(
                src_ref=src, dst_ref=dst, send_sem=send_sem.at[i], recv_sem=recv_sem.at[i],
                device_id=to, device_id_type=pl.DeviceIdType.MESH,
            )
        )
        sent.append(c)
        return c

    def finish():
        for c in sent:
            if not c.got:
                c.wait_recv()
        for c in sent:
            c.c.wait_send()
        for o in outs:
            o.wait()

    def step(i, n):
        return (i + n + 4) % 4

    sibling = (yh * 2 + (1 - core), col)
    partner = ((1 - yh) * 2 + core, col)

    barrier = pltpu.get_barrier_semaphore()
    peers = [dev(xi, zi, (q + n) % 8) for n in range(1, 8)]
    peers += [dev(step(xi, n), zi, q) for n in (1, 2, 3)]
    peers += [dev(xi, step(zi, n), q) for n in (1, 2, 3)]
    for p in peers:
        pl.semaphore_signal(barrier, inc=1, device_id=p, device_id_type=pl.DeviceIdType.MESH)

    w_in_copy = pltpu.make_async_copy(win_hbm, win, w_sem.at[0])
    w_out_copy = pltpu.make_async_copy(wout_hbm, wout, w_sem.at[1])
    w_in_copy.start()
    w_out_copy.start()

    xf = x_ref[...].astype(F32)
    cen = xf - jnp.mean(xf, axis=1, keepdims=True)
    inv = lax.rsqrt(jnp.mean(cen * cen, axis=1, keepdims=True) + 1e-05)
    nrm = (cen * inv * gain_ref[...]).astype(BF)
    for r in range(4):
        normed[r] = nrm[:, r * 2048 : (r + 1) * 2048]
    pl.semaphore_wait(barrier, len(peers))

    def column_in(src_of, dst):
        cs = []
        for n in range(1, 8):
            qq = (q + n) % 8
            cs.append(go(src_of(qq), dst.at[q], dev(xi, zi, qq)))
        return cs

    c0x = column_in(lambda qq: normed.at[qq // 2], s0x)
    c0g = column_in(
        lambda qq: og_ref.at[:, pl.ds(pl.multiple_of((qq // 2) * 2048, 2048), 2048)], s0g
    )
    s0x[q] = normed[row]
    s0g[q] = og_ref[:, pl.ds(pl.multiple_of(row * 2048, 2048), 2048)]

    pin = pin_ref[pl.ds(col * 2, 2), :]
    tile = lax.broadcasted_iota(jnp.int32, (8, 16), 0) + row * 8
    for h in range(2):
        kept = jnp.max(jnp.where(pin[h : h + 1] == tile, 1.0, 0.0), axis=1, keepdims=True)
        min_ref[:, h * 256 : (h + 1) * 256] = jnp.broadcast_to(kept, (8, 256))
    pout = pout_ref[pl.ds(pl.multiple_of(row * 8, 8), 8), :]
    for h in range(2):
        kept = jnp.max(jnp.where(pout == col * 2 + h, 1.0, 0.0), axis=1, keepdims=True)
        for t in range(8):
            mout_ref[h : h + 1, t * 256 : (t + 1) * 256] = jnp.broadcast_to(
                kept[t : t + 1], (1, 256)
            )

    def blk(g, k, u, v):
        return g.at[0, v, u] if k == 0 else g.at[1, u, v]

    def colours():
        st = []
        for k in range(2):
            u0, v0 = (zi, xi) if k == 0 else (xi, zi)

            def to_z(n):
                return dev(xi, step(zi, n), q)

            def to_x(n):
                return dev(step(xi, n), zi, q)

            st.append(
                dict(
                    k=k, u0=u0, v0=v0, to_u=to_z if k == 0 else to_x, to_v=to_x if k == 0 else to_z
                )
            )
        return st

    def gather(s0, g, arrived):
        for c in arrived:
            c.wait_recv()
        block = s0[...].reshape(64, 2048)
        g[0, xi, zi] = block[:, :1024]
        g[1, xi, zi] = block[:, 1024:]
        st = colours()

        def one(s, off, n, v=None):
            b = blk(g, s["k"], step(s["u0"], off), s["v0"] if v is None else v)
            return go(b, b, s["to_v"](n))

        def both(s, off):
            s["s", off] = {n: one(s, off, n) for n in (1, -1)}

        for s in st:
            b = blk(g, s["k"], s["u0"], s["v0"])
            s["f"] = {n: go(b, b, s["to_u"](n)) for n in (1, -1)}
            both(s, 0)
            s["f2"], s["s2"] = {}, {}
        yield
        for n in (1, -1):
            for s in st:
                s["f"][n].wait_recv()
                b = blk(g, s["k"], step(s["u0"], -n), s["v0"])
                part = b.at[pl.ds(0, 32)] if n == 1 else b.at[pl.ds(32, 32)]
                s["f2"][n] = go(part, part, s["to_u"](n))
                both(s, -n)
            yield

        def relay(s, off, n):
            s["s", off][n].wait_recv()
            s["s2"][off] = one(s, off, n, step(s["v0"], -n))

        for s in st:
            relay(s, 0, 1)
        yield
        for s in st:
            s["f2"][1].wait_recv()
            s["f2"][-1].wait_recv()
            both(s, 2)
        for s in st:
            s["s", 0][-1].wait_recv()
        yield
        for off in (-1, 1, 2):
            n = 1 if off == 1 else -1
            for s in st:
                relay(s, off, n)
            for s in st:
                s["s", off][-n].wait_recv()
            yield
        for off in (0, -1, 1, 2):
            for s in st:
                s["s2"][off].wait_recv()
            yield

    def drain(g, n):
        for _ in range(n):
            next(g, None)

    gen_x = gather(s0x, gx, c0x)
    gen_g = gather(s0g, gg, c0g)

    def partial(g, w, nt, xx):
        a = g[0, xx].reshape(256, 1024)
        b = g[1, xx].reshape(256, 1024)
        if nt:
            return dot_nt(a, w[:, :1024]) + dot_nt(b, w[:, 1024:])
        return dot_nn(a, w[:1024]) + dot_nn(b, w[1024:])

    def x_of(p, mine):
        c = core if mine else 1 - core
        return (xi + (4 - c if p == 0 else 1 + c)) % 4

    side = ((gx, win, False), (gg, wout, True))

    def row_other(i, p):
        ar_send[i, p] = partial(*side[i], x_of(p, False)).astype(BF)
        return go(ar_send.at[i, p], ar_recv.at[i, p], sibling)

    def row_mine(i, p):
        acc[i, p] = partial(*side[i], x_of(p, True))

    def row_add(i, p, c):
        c.wait_recv()
        v = acc[i, p] + ar_recv[i, p].astype(F32)
        acc[i, p] = v
        ay_send[i, p] = v.astype(BF)
        return go(ay_send.at[i, p], ay_recv.at[i, p], partner)

    def rows_loop(f):
        def body(m, _):
            f(m, pl.ds(pl.multiple_of(m * 64, 64), 64))
            return 0

        lax.fori_loop(0, 4, body, 0)

    def row_act(p, c):
        c.wait_recv()
        xx = x_of(p, True)

        def rows_of(m, rows):
            pre = acc[0, p, rows] + ay_recv[0, p, rows].astype(F32)
            acc[0, p, rows] = pre
            act[xx, m] = gelu_value(pre).astype(BF)

        rows_loop(rows_of)
        return go(act.at[xx], act.at[xx], sibling)

    def row_dpre(p, c):
        c.wait_recv()
        xx = x_of(p, True)

        def rows_of(m, rows):
            d = acc[1, p, rows] + ay_recv[1, p, rows].astype(F32)
            dpre[xx, m] = (d * gelu_slope(acc[0, p, rows])).astype(BF)

        rows_loop(rows_of)
        return go(dpre.at[xx], dpre.at[xx], sibling)

    def term(t, k, v):
        if t == 0:
            a = act[v] if k == 0 else act[:, v]
            r = dot_nn(a.reshape(256, 512), wout[:, k * 1024 : (k + 1) * 1024])
        else:
            a = dpre[v] if k == 0 else dpre[:, v]
            r = dot_nt(a.reshape(256, 512), win[k * 1024 : (k + 1) * 1024, :])
        return r.reshape(4, 64, 1024)

    last = {}

    def scatter(t):
        st = colours()
        with_half = {1: (2, -1), -1: (1, 0)}
        for s in st:
            k = s["k"]
            rs_far[t, k] = term(t, k, step(s["v0"], 2)).astype(BF)
            s["h"], s["w"], s["uw"] = {}, {}, {}
            for i in range(2):
                for n in (1, -1):
                    off = with_half[n][i]
                    u = step(s["u0"], off)
                    s["h"][off] = go(rs_far.at[t, k, u], rs_half.at[t, k, u], s["to_v"](n))
        yield

        def piece(s, n, off):
            k, u, j = s["k"], step(s["u0"], off), 0 if n == 1 else 1
            p = rs_p[k, j, u]
            if off in with_half[n]:
                s["h"][off].wait_recv()
                p = p + rs_half[t, k, u].astype(F32)
            rs_full[t, k, j, u] = p.astype(BF)
            s["w"][n, off] = go(rs_full.at[t, k, j, u], rs_in.at[t, k, j, u], s["to_v"](n))

        for n in (-1, 1):
            for s in st:
                rs_p[s["k"], 0 if n == 1 else 1] = term(t, s["k"], step(s["v0"], n))
                for off in with_half[-n]:
                    piece(s, n, off)
        yield
        for i in range(2):
            for n in (1, -1):
                for s in st:
                    piece(s, n, with_half[n][i])
        yield
        for s in st:
            rs_p[s["k"], 2] = term(t, s["k"], s["v0"])
        yield

        def summed(s, off):
            k, u = s["k"], step(s["u0"], off)
            s["w"][1, off].wait_recv()
            s["w"][-1, off].wait_recv()
            return rs_p[k, 2, u] + rs_in[t, k, 0, u].astype(F32) + rs_in[t, k, 1, u].astype(F32)

        for s in st:
            k = s["k"]
            ru_far[t, k] = summed(s, 2).astype(BF)
            s["uh"] = {
                n: go(
                    ru_far.at[t, k, pl.ds(0 if n == 1 else 32, 32)],
                    ru_half.at[t, k, 0 if n == 1 else 1],
                    s["to_u"](n),
                )
                for n in (1, -1)
            }
        yield
        for n in (-1, 1):
            for s in st:
                k, j = s["k"], 0 if n == 1 else 1
                p = summed(s, n)
                s["uh"][n].wait_recv()
                extra = ru_half[t, k, j].astype(F32)
                lo, hi = p[0:32], p[32:64]
                if n == 1:
                    lo = lo + extra
                else:
                    hi = hi + extra
                ru_full[t, k, j, 0:32] = lo.astype(BF)
                ru_full[t, k, j, 32:64] = hi.astype(BF)
                s["uw"][n] = go(ru_full.at[t, k, j], ru_in.at[t, k, j], s["to_u"](n))
        yield
        for s in st:
            k = s["k"]
            r = summed(s, 0)
            s["uw"][1].wait_recv()
            s["uw"][-1].wait_recv()
            r = r + ru_in[t, k, 0].astype(F32) + ru_in[t, k, 1].astype(F32)
            rfin[t, :, :, k * 1024 : (k + 1) * 1024] = r.astype(BF).reshape(8, 8, 1024)
        last[t] = [
            go(rfin.at[t, (q + n) % 8], e_buf.at[t, q], dev(xi, zi, (q + n) % 8))
            for n in range(1, 8)
        ]
        e_buf[t, q] = rfin[t, q]
        yield

    ones = jnp.ones((8, 512), BF)

    def grad_in_tiles(k, lo, hi):
        def win_tile(j, _):
            lanes = pl.ds(pl.multiple_of(j * 256, 256), 256)
            ft = k * 4 + j
            a = gx[k, :, :, :, lanes].reshape(1024, 256)
            raw = dot_tn(a, dpre[...].reshape(1024, 512))
            rows = pl.ds(pl.multiple_of(ft * 256, 256), 256)
            gw1[rows] = (raw * min_ref[pl.ds(ft, 1)]).astype(BF)
            p = raw * win[rows].astype(F32)
            hi = p.astype(BF)
            lo = (p - hi.astype(F32)).astype(BF)
            s = dot_nt(ones, hi) + dot_nt(ones, lo)
            s_x[xi, pl.ds(2 * ft, 1)] = s[0:1, :128]
            s_x[xi, pl.ds(2 * ft + 1, 1)] = s[0:1, 128:]
            return 0

        lax.fori_loop(lo, hi, win_tile, 0)

    def grad_out_tiles(k, lo, hi):
        def wout_tile(j, _):
            lanes = pl.ds(pl.multiple_of(j * 256, 256), 256)
            b = gg[k, :, :, :, lanes].reshape(1024, 256)
            raw = dot_tn(act[...].reshape(1024, 512), b)
            cols = pl.ds(pl.multiple_of(k * 1024 + j * 256, 256), 256)
            for h in range(2):
                gw2[h * 256 : (h + 1) * 256, cols] = (
                    raw[h * 256 : (h + 1) * 256] * mout_ref[h : h + 1, cols]
                ).astype(BF)
            return 0

        lax.fori_loop(lo, hi, wout_tile, 0)

    def put(src, dst, i):
        o = pltpu.make_async_copy(src, dst, w_sem.at[i])
        o.start()
        outs.append(o)

    drain(gen_x, 1)
    w_in_copy.wait()
    for t in range(8):
        win[t * 256 : (t + 1) * 256] = win[t * 256 : (t + 1) * 256] * min_ref[t : t + 1].astype(BF)
    w_out_copy.wait()
    drain(gen_x, 4)
    drain(gen_g, 1)
    for t in range(2):
        wout[t * 256 : (t + 1) * 256] = wout[t * 256 : (t + 1) * 256] * mout_ref[t : t + 1].astype(BF)
    drain(gen_x, 2)
    drain(gen_g, 1)
    drain(gen_x, 1)
    drain(gen_g, 1)
    drain(gen_x, 2)
    ca0 = row_other(0, 0)
    row_mine(0, 0)
    drain(gen_g, 1)
    cb0 = row_add(0, 0, ca0)
    drain(gen_x, 2)
    ca1 = row_other(0, 1)
    row_mine(0, 1)
    cb1 = row_add(0, 1, ca1)
    drain(gen_g, 3)
    cc0 = row_act(0, cb0)
    drain(gen_g, 1)
    cc1 = row_act(1, cb1)
    cc0.wait_recv()
    cc1.wait_recv()
    gen_o = scatter(0)
    drain(gen_o, 1)
    drain(gen_g, 2)
    da0 = row_other(1, 0)
    drain(gen_o, 1)
    row_mine(1, 0)
    db0 = row_add(1, 0, da0)
    drain(gen_g, 2)
    da1 = row_other(1, 1)
    row_mine(1, 1)
    db1 = row_add(1, 1, da1)
    drain(gen_o, 2)
    grad_out_tiles(0, 0, 4)
    dc0 = row_dpre(0, db0)
    drain(gen_o, 1)
    grad_out_tiles(1, 0, 4)
    put(gw2, gwout_ref, 1)
    dc1 = row_dpre(1, db1)
    drain(gen_o, 1)
    dc0.wait_recv()
    dc1.wait_recv()
    gen_d = scatter(1)
    drain(gen_d, 2)
    drain(gen_o, 1)
    grad_in_tiles(0, 0, 2)
    drain(gen_d, 1)
    grad_in_tiles(0, 2, 4)
    drain(gen_d, 1)
    grad_in_tiles(1, 0, 4)
    put(gw1, gwin_ref, 0)
    sx = [go(s_x.at[xi], s_x.at[xi], dev(step(xi, n), zi, q)) for n in (1, 2, 3)]
    drain(gen_d, 1)
    for c in last[0]:
        c.wait_recv()
    for r in range(4):
        f = slice(r * 2048, (r + 1) * 2048)
        o = e_buf[0, 2 * r].astype(F32) + e_buf[0, 2 * r + 1].astype(F32)
        out_ref[:, f] = (x_ref[:, f].astype(F32) + o).astype(BF)
    for c in sx:
        c.wait_recv()
    s_z[zi] = (s_x[0] + s_x[1]) + (s_x[2] + s_x[3])
    sz = [go(s_z.at[zi], s_z.at[zi], dev(xi, step(zi, n), q)) for n in (1, 2, 3)]
    drain(gen_d, 1)
    for c in sz:
        c.wait_recv()
    s_c[q] = (s_z[0] + s_z[1]) + (s_z[2] + s_z[3])
    sc = [go(s_c.at[q], s_c.at[q], dev(xi, zi, (q + n) % 8)) for n in range(1, 8)]
    drain(gen_d, 1)
    for c in sc:
        c.wait_recv()
    for r in range(4):
        gg_ref[r * 16 : (r + 1) * 16] = (s_c[2 * r] + s_c[2 * r + 1]) / gain64_ref[r * 16 : (r + 1) * 16]
    xf = x_ref[...].astype(F32)
    cen = xf - jnp.mean(xf, axis=1, keepdims=True)
    inv = lax.rsqrt(jnp.mean(cen * cen, axis=1, keepdims=True) + 1e-05)
    hat = cen * inv
    for c in last[1]:
        c.wait_recv()
    parts = [
        e_buf[1, 2 * r].astype(F32) + e_buf[1, 2 * r + 1].astype(F32) for r in range(4)
    ]
    d = jnp.concatenate(parts, axis=1)
    g = d * gain_ref[...]
    back = inv * (
        g - jnp.mean(g, axis=1, keepdims=True) - hat * jnp.mean(g * hat, axis=1, keepdims=True)
    )
    gin_ref[...] = (og_ref[...].astype(F32) + back).astype(BF)
    finish()


def hand_over(n, *refs):
    ins, outs, bufs = refs[:n], refs[n : 2 * n], refs[2 * n : 3 * n]
    sem_in, sem_out = refs[3 * n :]
    moves, i = [], 0
    for a, o, b in zip(ins, outs, bufs):
        parts = 4 if a.shape[0] > 64 else 1
        rows = a.shape[0] // parts
        for p in range(parts):
            r = pl.ds(p * rows, rows)
            moves.append(
                (
                    pltpu.make_async_copy(a.at[r], b.at[r], sem_in.at[i]),
                    pltpu.make_async_copy(b.at[r], o.at[r], sem_out.at[i]),
                )
            )
            i += 1
    for get, _ in moves:
        get.start()
    for get, give in moves:
        get.wait()
        give.start()
    for _, give in moves:
        give.wait()


def shards(inputs, layer_norm_gain, w_in, w_out, pattern_in, pattern_out, out_grad):
    vm = functools.partial(pl.BlockSpec, memory_space=pltpu.VMEM)
    hbm = functools.partial(pl.BlockSpec, memory_space=pl.ANY)
    V = pltpu.VMEM
    out = pl.pallas_call(
        kernel,
        out_shape=(
            jax.ShapeDtypeStruct((8, 8192), BF),
            jax.ShapeDtypeStruct((8, 8192), BF),
            jax.ShapeDtypeStruct((2048, 512), BF),
            jax.ShapeDtypeStruct((512, 2048), BF),
            jax.ShapeDtypeStruct((64, 128), F32),
        ),
        in_specs=[vm(), vm(), vm(), vm(), hbm(), hbm(), vm(), vm()],
        out_specs=(vm(), vm(), hbm(), hbm(), vm()),
        scratch_shapes=[
            V((2048, 512), BF),
            V((512, 2048), BF),
            V((8, 512), F32),
            V((2, 2048), F32),
            V((4, 8, 2048), BF),
            V((8, 8, 2048), BF),
            V((8, 8, 2048), BF),
            V((2, 4, 4, 64, 1024), BF),
            V((2, 4, 4, 64, 1024), BF),
            V((2, 2, 256, 512), BF),
            V((2, 2, 256, 512), BF),
            V((2, 2, 256, 512), BF),
            V((2, 2, 256, 512), BF),
            V((2, 2, 256, 512), F32),
            V((4, 4, 64, 512), BF),
            V((4, 4, 64, 512), BF),
            V((2, 2, 4, 64, 1024), BF),
            V((2, 2, 4, 64, 1024), BF),
            V((2, 2, 2, 4, 64, 1024), BF),
            V((2, 2, 2, 4, 64, 1024), BF),
            V((2, 3, 4, 64, 1024), F32),
            V((2, 2, 64, 1024), BF),
            V((2, 2, 2, 32, 1024), BF),
            V((2, 2, 2, 64, 1024), BF),
            V((2, 2, 2, 64, 1024), BF),
            V((2, 8, 8, 2048), BF),
            V((2, 8, 8, 2048), BF),
            V((2048, 512), BF),
            V((512, 2048), BF),
            V((4, 16, 128), F32),
            V((4, 16, 128), F32),
            V((8, 16, 128), F32),
            pltpu.SemaphoreType.DMA((N_COPIES,)),
            pltpu.SemaphoreType.DMA((N_COPIES,)),
            pltpu.SemaphoreType.DMA((2,)),
        ],
        compiler_params=pltpu.CompilerParams(
            collective_id=0, has_side_effects=True, vmem_limit_bytes=67_043_328
        ),
        name="ffn",
    )(
        inputs, layer_norm_gain.reshape(1, 8192), layer_norm_gain.reshape(64, 128), out_grad,
        w_in, w_out, pattern_in, pattern_out,
    )
    output, grad_inputs, g_in, g_out, g_gain = pl.pallas_call(
        functools.partial(hand_over, len(out)),
        out_shape=tuple(jax.ShapeDtypeStruct(o.shape, o.dtype) for o in out),
        in_specs=[hbm()] * len(out),
        out_specs=(hbm(),) * len(out),
        scratch_shapes=[V(o.shape, o.dtype) for o in out]
        + [pltpu.SemaphoreType.DMA((16,)), pltpu.SemaphoreType.DMA((16,))],
        name="hand_over",
    )(*out)
    return output, grad_inputs, g_in, g_out, g_gain.reshape(8192)


def solution(mesh):
    in_specs = (
        P(("row", "col"), None),
        P(),
        P("row", "col"),
        P("col", "row"),
        P(),
        P(),
        P(("row", "col"), None),
    )
    out_specs = (
        P(("row", "col"), None),
        P(("row", "col"), None),
        P("row", "col"),
        P("col", "row"),
        P(),
    )
    return jax.shard_map(shards, mesh=mesh, in_specs=in_specs, out_specs=out_specs, check_vma=False)
```

time: 160 us -> 130 us (0.81)
  Pallas kernels: 147 us -> 127 us
  local copies, waits for them, and re-layouts: 9.81 us -> 1.39 us
  other arithmetic: 1.88 us -> 0 us
    pallas_call x1, Pallas kernels: 147 us -> 123 us  [shards(): pl.pallas_call(kernel, out_shape=(jax.ShapeDtypeStruct((8, 8192), BF), ja...]
    unnamed x11 -> x1, local copies, waits for them, and re-layouts: 8.96 us -> 1.39 us
    pallas_call x0 -> x1, Pallas kernels: none -> 4.17 us  [shards(): pl.pallas_call(functools.partial(hand_over, len(out)), out_shape=tuple((j...]
    reduce_or x2 -> x0, other arithmetic: 1.71 us -> none  [tile_mask(): return jnp.any(pattern[None, :, :] == iota[:, None, None], axis=2)]
where the time goes in v2:
time: 130 us
  Pallas kernels  127 us (98%)
  local copies, waits for them, and re-layouts  1.39 us (1%)
    pallas_call x1, Pallas kernels, shards(): pl.pallas_call(kernel, out_shape=(jax.ShapeDtypeStruct((8, 8192), BF), ja...  123 us
    pallas_call x1, Pallas kernels, shards(): pl.pallas_call(functools.partial(hand_over, len(out)), out_shape=tuple((j...  4.17 us

profile of v2, /device:TPU:1, one launch (start us, length us, event | category | flops | bytes accessed | tf_op | source)
XLA Modules:
  0.0 129.5 jit_solution(1110534844750752899)
XLA Ops:
  0.6 1.4 %copy.12.pin_ref = s32[64,16]{1,0:T(8,128)} copy(s32[64,16]{0,1:T(8,128)} %param.11) | data formatting | bytes 8192 | tf_op args[4]
  2.0 123.2 %ffn.1 = (bf16[8,8192]{1,0:T(8,128)(2,1)}, bf16[8,8192]{1,0:T(8,128)(2,1)}, bf16[2048,512]{1,0:T(8,128)(2,1)}, bf16[512,2048]{1,0:T(8,128)(2,1)}, f32[64,128]{1,0:T(8,128)}) custom-call(bf16[8,8192]{1,0:T(8,128)(2,1)} %x_ref.1, f32[1,8192]{1,0:T(1,128)} %bitcast.3, f32[64,128]{1,0:T(8,128)} %bitcast.4, bf16[8,8192]{1,0:T(8,128)(2,1)} %og_ref.1, ...), custom_call_target="tpu_custom_call" | custom-call | tf_op jit(solution)/shard_map/ffn/pallas_call | solution.py:547
  125.2 4.2 %hand_over.1 = (bf16[8,8192]{1,0:T(8,128)(2,1)}, bf16[8,8192]{1,0:T(8,128)(2,1)}, bf16[2048,512]{1,0:T(8,128)(2,1)}, bf16[512,2048]{1,0:T(8,128)(2,1)}, f32[64,128]{1,0:T(8,128)}) custom-call(bf16[8,8192]{1,0:T(8,128)(2,1)} %get-tuple-element.15.refs_0_, bf16[8,8192]{1,0:T(8,128)(2,1)} %get-tuple-element.16.refs_1_, ...), custom_call_target="tpu_custom_call" | custom-call | tf_op jit(solution)/shard_map/hand_over/pallas_call | solution.py:603

commit v3 on v2

--- a/solution.py
+++ b/solution.py
@@ -122,17 +122,18 @@
         return cs
 
     c0x = column_in(lambda qq: normed.at[qq // 2], s0x)
-    c0g = column_in(
-        lambda qq: og_ref.at[:, pl.ds(pl.multiple_of((qq // 2) * 2048, 2048), 2048)], s0g
-    )
     s0x[q] = normed[row]
     s0g[q] = og_ref[:, pl.ds(pl.multiple_of(row * 2048, 2048), 2048)]
 
-    pin = pin_ref[pl.ds(col * 2, 2), :]
-    tile = lax.broadcasted_iota(jnp.int32, (8, 16), 0) + row * 8
+    lane = lax.broadcasted_iota(jnp.int32, (16, 64), 1)
+    tile = lax.broadcasted_iota(jnp.int32, (16, 128), 1) + row * 8
     for h in range(2):
-        kept = jnp.max(jnp.where(pin[h : h + 1] == tile, 1.0, 0.0), axis=1, keepdims=True)
-        min_ref[:, h * 256 : (h + 1) * 256] = jnp.broadcast_to(kept, (8, 256))
+        rows = jnp.max(jnp.where(lane == col * 2 + h, pin_ref[...], -1), axis=1, keepdims=True)
+        kept = jnp.max(jnp.where(rows == tile, 1.0, 0.0), axis=0, keepdims=True)
+        for t in range(8):
+            min_ref[t : t + 1, h * 256 : (h + 1) * 256] = jnp.broadcast_to(
+                kept[:, t : t + 1], (1, 256)
+            )
     pout = pout_ref[pl.ds(pl.multiple_of(row * 8, 8), 8), :]
     for h in range(2):
         kept = jnp.max(jnp.where(pout == col * 2 + h, 1.0, 0.0), axis=1, keepdims=True)
@@ -223,6 +224,7 @@
             next(g, None)
 
     gen_x = gather(s0x, gx, c0x)
+    c0g = []
     gen_g = gather(s0g, gg, c0g)
 
     def partial(g, w, nt, xx):
@@ -316,17 +318,18 @@
             rs_full[t, k, j, u] = p.astype(BF)
             s["w"][n, off] = go(rs_full.at[t, k, j, u], rs_in.at[t, k, j, u], s["to_v"](n))
 
-        for n in (-1, 1):
+        for n, off in ((-1, 2), (1, 1)):
             for s in st:
                 rs_p[s["k"], 0 if n == 1 else 1] = term(t, s["k"], step(s["v0"], n))
-                for off in with_half[-n]:
-                    piece(s, n, off)
-        yield
-        for i in range(2):
-            for n in (1, -1):
-                for s in st:
-                    piece(s, n, with_half[n][i])
-        yield
+                piece(s, n, off)
+        yield
+        for n, off in ((-1, -1), (1, 2)):
+            for s in st:
+                piece(s, n, off)
+        yield
+        for n, off in ((-1, 1), (1, -1)):
+            for s in st:
+                piece(s, n, off)
         for s in st:
             rs_p[s["k"], 2] = term(t, s["k"], s["v0"])
         yield
@@ -348,6 +351,9 @@
                 )
                 for n in (1, -1)
             }
+        for s in st:
+            for n in (1, -1):
+                piece(s, n, 0)
         yield
         for n in (-1, 1):
             for s in st:
@@ -418,6 +424,9 @@
         outs.append(o)
 
     drain(gen_x, 1)
+    c0g += column_in(
+        lambda qq: og_ref.at[:, pl.ds(pl.multiple_of((qq // 2) * 2048, 2048), 2048)], s0g
+    )
     w_in_copy.wait()
     for t in range(8):
         win[t * 256 : (t + 1) * 256] = win[t * 256 : (t + 1) * 256] * min_ref[t : t + 1].astype(BF)
@@ -431,17 +440,17 @@
     drain(gen_x, 1)
     drain(gen_g, 1)
     drain(gen_x, 2)
+    drain(gen_g, 2)
     ca0 = row_other(0, 0)
     row_mine(0, 0)
-    drain(gen_g, 1)
     cb0 = row_add(0, 0, ca0)
     drain(gen_x, 2)
+    drain(gen_g, 1)
     ca1 = row_other(0, 1)
     row_mine(0, 1)
     cb1 = row_add(0, 1, ca1)
-    drain(gen_g, 3)
+    drain(gen_g, 2)
     cc0 = row_act(0, cb0)
-    drain(gen_g, 1)
     cc1 = row_act(1, cb1)
     cc0.wait_recv()
     cc1.wait_recv()
@@ -454,35 +463,37 @@
     db0 = row_add(1, 0, da0)
     drain(gen_g, 2)
     da1 = row_other(1, 1)
+    drain(gen_o, 1)
     row_mine(1, 1)
     db1 = row_add(1, 1, da1)
-    drain(gen_o, 2)
+    drain(gen_o, 1)
     grad_out_tiles(0, 0, 4)
     dc0 = row_dpre(0, db0)
     drain(gen_o, 1)
-    grad_out_tiles(1, 0, 4)
-    put(gw2, gwout_ref, 1)
     dc1 = row_dpre(1, db1)
-    drain(gen_o, 1)
     dc0.wait_recv()
     dc1.wait_recv()
     gen_d = scatter(1)
-    drain(gen_d, 2)
+    drain(gen_d, 1)
     drain(gen_o, 1)
-    grad_in_tiles(0, 0, 2)
     drain(gen_d, 1)
-    grad_in_tiles(0, 2, 4)
+    drain(gen_o, 1)
+    drain(gen_d, 1)
+    grad_out_tiles(1, 0, 4)
+    put(gw2, gwout_ref, 1)
+    drain(gen_d, 1)
+    grad_in_tiles(0, 0, 4)
     drain(gen_d, 1)
     grad_in_tiles(1, 0, 4)
     put(gw1, gwin_ref, 0)
     sx = [go(s_x.at[xi], s_x.at[xi], dev(step(xi, n), zi, q)) for n in (1, 2, 3)]
-    drain(gen_d, 1)
     for c in last[0]:
         c.wait_recv()
     for r in range(4):
         f = slice(r * 2048, (r + 1) * 2048)
         o = e_buf[0, 2 * r].astype(F32) + e_buf[0, 2 * r + 1].astype(F32)
         out_ref[:, f] = (x_ref[:, f].astype(F32) + o).astype(BF)
+    drain(gen_d, 1)
     for c in sx:
         c.wait_recv()
     s_z[zi] = (s_x[0] + s_x[1]) + (s_x[2] + s_x[3])
@@ -492,7 +503,6 @@
         c.wait_recv()
     s_c[q] = (s_z[0] + s_z[1]) + (s_z[2] + s_z[3])
     sc = [go(s_c.at[q], s_c.at[q], dev(xi, zi, (q + n) % 8)) for n in range(1, 8)]
-    drain(gen_d, 1)
     for c in sc:
         c.wait_recv()
     for r in range(4):
@@ -598,7 +608,7 @@
         name="ffn",
     )(
         inputs, layer_norm_gain.reshape(1, 8192), layer_norm_gain.reshape(64, 128), out_grad,
-        w_in, w_out, pattern_in, pattern_out,
+        w_in, w_out, pattern_in.T, pattern_out,
     )
     output, grad_inputs, g_in, g_out, g_gain = pl.pallas_call(
         functools.partial(hand_over, len(out)),

time: 130 us -> 134 us (1.031)
  Pallas kernels: 127 us -> 133 us
  local copies, waits for them, and re-layouts: 1.39 us -> 0 us
    pallas_call x1, Pallas kernels: 123 us -> 129 us  [shards(): pl.pallas_call(kernel, out_shape=(jax.ShapeDtypeStruct((8, 8192), BF), ja...]
    unnamed x1 -> x0, local copies, waits for them, and re-layouts: 1.39 us -> none
where the time goes in v3:
time: 134 us
  Pallas kernels  133 us (99%)
    pallas_call x1, Pallas kernels, shards(): pl.pallas_call(kernel, out_shape=(jax.ShapeDtypeStruct((8, 8192), BF), ja...  129 us
    pallas_call x1, Pallas kernels, shards(): pl.pallas_call(functools.partial(hand_over, len(out)), out_shape=tuple((j...  4.17 us

profile of v3, /device:TPU:1, one launch (start us, length us, event | category | flops | bytes accessed | tf_op | source)
XLA Modules:
  0.0 134.2 jit_solution(6740536672486803695)
XLA Ops:
  0.6 129.2 %ffn.1 = (bf16[8,8192]{1,0:T(8,128)(2,1)}, bf16[8,8192]{1,0:T(8,128)(2,1)}, bf16[2048,512]{1,0:T(8,128)(2,1)}, bf16[512,2048]{1,0:T(8,128)(2,1)}, f32[64,128]{1,0:T(8,128)}) custom-call(bf16[8,8192]{1,0:T(8,128)(2,1)} %x_ref.1, f32[1,8192]{1,0:T(1,128)} %bitcast.4, f32[64,128]{1,0:T(8,128)} %bitcast.5, bf16[8,8192]{1,0:T(8,128)(2,1)} %og_ref.1, ...), custom_call_target="tpu_custom_call" | custom-call | tf_op jit(solution)/shard_map/ffn/pallas_call | solution.py:557
  129.8 4.2 %hand_over.1 = (bf16[8,8192]{1,0:T(8,128)(2,1)}, bf16[8,8192]{1,0:T(8,128)(2,1)}, bf16[2048,512]{1,0:T(8,128)(2,1)}, bf16[512,2048]{1,0:T(8,128)(2,1)}, f32[64,128]{1,0:T(8,128)}) custom-call(bf16[8,8192]{1,0:T(8,128)(2,1)} %get-tuple-element.15.refs_0_, bf16[8,8192]{1,0:T(8,128)(2,1)} %get-tuple-element.16.refs_1_, ...), custom_call_target="tpu_custom_call" | custom-call | tf_op jit(solution)/shard_map/hand_over/pallas_call | solution.py:613

commit v4 on v3

--- a/solution.py
+++ b/solution.py
@@ -431,27 +431,25 @@
     for t in range(8):
         win[t * 256 : (t + 1) * 256] = win[t * 256 : (t + 1) * 256] * min_ref[t : t + 1].astype(BF)
     w_out_copy.wait()
-    drain(gen_x, 4)
-    drain(gen_g, 1)
     for t in range(2):
         wout[t * 256 : (t + 1) * 256] = wout[t * 256 : (t + 1) * 256] * mout_ref[t : t + 1].astype(BF)
-    drain(gen_x, 2)
-    drain(gen_g, 1)
-    drain(gen_x, 1)
+    drain(gen_x, 7)
     drain(gen_g, 1)
     drain(gen_x, 2)
-    drain(gen_g, 2)
     ca0 = row_other(0, 0)
     row_mine(0, 0)
+    drain(gen_g, 2)
     cb0 = row_add(0, 0, ca0)
     drain(gen_x, 2)
+    ca1 = row_other(0, 1)
     drain(gen_g, 1)
-    ca1 = row_other(0, 1)
     row_mine(0, 1)
     cb1 = row_add(0, 1, ca1)
     drain(gen_g, 2)
     cc0 = row_act(0, cb0)
+    drain(gen_g, 1)
     cc1 = row_act(1, cb1)
+    drain(gen_g, 1)
     cc0.wait_recv()
     cc1.wait_recv()
     gen_o = scatter(0)
@@ -463,12 +461,13 @@
     db0 = row_add(1, 0, da0)
     drain(gen_g, 2)
     da1 = row_other(1, 1)
-    drain(gen_o, 1)
     row_mine(1, 1)
     db1 = row_add(1, 1, da1)
+    drain(gen_o, 2)
+    grad_out_tiles(0, 0, 2)
+    dc0 = row_dpre(0, db0)
     drain(gen_o, 1)
-    grad_out_tiles(0, 0, 4)
-    dc0 = row_dpre(0, db0)
+    grad_out_tiles(0, 2, 4)
     drain(gen_o, 1)
     dc1 = row_dpre(1, db1)
     dc0.wait_recv()
@@ -477,9 +476,9 @@
     drain(gen_d, 1)
     drain(gen_o, 1)
     drain(gen_d, 1)
-    drain(gen_o, 1)
+    grad_out_tiles(1, 0, 2)
     drain(gen_d, 1)
-    grad_out_tiles(1, 0, 4)
+    grad_out_tiles(1, 2, 4)
     put(gw2, gwout_ref, 1)
     drain(gen_d, 1)
     grad_in_tiles(0, 0, 4)

time: 134 us -> 121 us (0.903)
  Pallas kernels: 133 us -> 120 us
    pallas_call x1, Pallas kernels: 129 us -> 116 us  [shards(): pl.pallas_call(kernel, out_shape=(jax.ShapeDtypeStruct((8, 8192), BF), ja...]
where the time goes in v4:
time: 121 us
  Pallas kernels  120 us (99%)
    pallas_call x1, Pallas kernels, shards(): pl.pallas_call(kernel, out_shape=(jax.ShapeDtypeStruct((8, 8192), BF), ja...  116 us
    pallas_call x1, Pallas kernels, shards(): pl.pallas_call(functools.partial(hand_over, len(out)), out_shape=tuple((j...  4.17 us

profile of v4, /device:TPU:1, one launch (start us, length us, event | category | flops | bytes accessed | tf_op | source)
XLA Modules:
  0.0 120.6 jit_solution(15722500128439269800)
XLA Ops:
  0.6 115.7 %ffn.1 = (bf16[8,8192]{1,0:T(8,128)(2,1)}, bf16[8,8192]{1,0:T(8,128)(2,1)}, bf16[2048,512]{1,0:T(8,128)(2,1)}, bf16[512,2048]{1,0:T(8,128)(2,1)}, f32[64,128]{1,0:T(8,128)}) custom-call(bf16[8,8192]{1,0:T(8,128)(2,1)} %x_ref.1, f32[1,8192]{1,0:T(1,128)} %bitcast.4, f32[64,128]{1,0:T(8,128)} %bitcast.5, bf16[8,8192]{1,0:T(8,128)(2,1)} %og_ref.1, ...), custom_call_target="tpu_custom_call" | custom-call | tf_op jit(solution)/shard_map/ffn/pallas_call | solution.py:556
  116.3 4.2 %hand_over.1 = (bf16[8,8192]{1,0:T(8,128)(2,1)}, bf16[8,8192]{1,0:T(8,128)(2,1)}, bf16[2048,512]{1,0:T(8,128)(2,1)}, bf16[512,2048]{1,0:T(8,128)(2,1)}, f32[64,128]{1,0:T(8,128)}) custom-call(bf16[8,8192]{1,0:T(8,128)(2,1)} %get-tuple-element.15.refs_0_, bf16[8,8192]{1,0:T(8,128)(2,1)} %get-tuple-element.16.refs_1_, ...), custom_call_target="tpu_custom_call" | custom-call | tf_op jit(solution)/shard_map/hand_over/pallas_call | solution.py:612

commit v5 on v4

--- a/solution.py
+++ b/solution.py
@@ -10,6 +10,7 @@
 BF = jnp.bfloat16
 F32 = jnp.float32
 N_COPIES = 256
+FAR_FIRST = ((1, 0, 0), (1, 1, 0), (0, 0, 1), (0, 1, 1), (1, 0, 1), (1, 1, 1), (0, 1, 0))
 
 
 def gelu_value(h):
@@ -48,12 +49,12 @@
 
 def kernel(
     x_ref, gain_ref, gain64_ref, og_ref, win_hbm, wout_hbm, pin_ref, pout_ref,
-    out_ref, gin_ref, gwin_ref, gwout_ref, gg_ref,
+    out_ref, gin_ref, gw1, gw2, gg_ref,
     win, wout, min_ref, mout_ref, normed, s0x, s0g, gx, gg,
     ar_send, ar_recv, ay_send, ay_recv, acc, act, dpre,
     rs_far, rs_half, rs_full, rs_in, rs_p,
     ru_far, ru_half, ru_full, ru_in,
-    rfin, e_buf, gw1, gw2, s_x, s_z, s_c,
+    rfin, e_buf, s_x, s_z, s_c,
     send_sem, recv_sem, w_sem,
 ):
     row = lax.axis_index("row")
@@ -66,7 +67,6 @@
         return (qq // 2, (x * 4 + z) * 2 + qq % 2)
 
     sent = []
-    outs = []
 
     def go(src, dst, to):
         i = len(sent)
@@ -85,14 +85,17 @@
                 c.wait_recv()
         for c in sent:
             c.c.wait_send()
-        for o in outs:
-            o.wait()
 
     def step(i, n):
         return (i + n + 4) % 4
 
+    def flip(h, c, y):
+        return (yh + h) % 2 * 4 + (core + c) % 2 * 2 + (yl + y) % 2
+
     sibling = (yh * 2 + (1 - core), col)
     partner = ((1 - yh) * 2 + core, col)
+
+    far_first = [flip(h, c, y) for h, c, y in FAR_FIRST]
 
     barrier = pltpu.get_barrier_semaphore()
     peers = [dev(xi, zi, (q + n) % 8) for n in range(1, 8)]
@@ -116,8 +119,7 @@
 
     def column_in(src_of, dst):
         cs = []
-        for n in range(1, 8):
-            qq = (q + n) % 8
+        for qq in far_first:
             cs.append(go(src_of(qq), dst.at[q], dev(xi, zi, qq)))
         return cs
 
@@ -378,8 +380,7 @@
             r = r + ru_in[t, k, 0].astype(F32) + ru_in[t, k, 1].astype(F32)
             rfin[t, :, :, k * 1024 : (k + 1) * 1024] = r.astype(BF).reshape(8, 8, 1024)
         last[t] = [
-            go(rfin.at[t, (q + n) % 8], e_buf.at[t, q], dev(xi, zi, (q + n) % 8))
-            for n in range(1, 8)
+            go(rfin.at[t, qq], e_buf.at[t, q], dev(xi, zi, qq)) for qq in far_first
         ]
         e_buf[t, q] = rfin[t, q]
         yield
@@ -417,11 +418,6 @@
             return 0
 
         lax.fori_loop(lo, hi, wout_tile, 0)
-
-    def put(src, dst, i):
-        o = pltpu.make_async_copy(src, dst, w_sem.at[i])
-        o.start()
-        outs.append(o)
 
     drain(gen_x, 1)
     c0g += column_in(
@@ -479,12 +475,10 @@
     grad_out_tiles(1, 0, 2)
     drain(gen_d, 1)
     grad_out_tiles(1, 2, 4)
-    put(gw2, gwout_ref, 1)
     drain(gen_d, 1)
     grad_in_tiles(0, 0, 4)
     drain(gen_d, 1)
     grad_in_tiles(1, 0, 4)
-    put(gw1, gwin_ref, 0)
     sx = [go(s_x.at[xi], s_x.at[xi], dev(step(xi, n), zi, q)) for n in (1, 2, 3)]
     for c in last[0]:
         c.wait_recv()
@@ -525,28 +519,12 @@
 
 
 def hand_over(n, *refs):
-    ins, outs, bufs = refs[:n], refs[n : 2 * n], refs[2 * n : 3 * n]
-    sem_in, sem_out = refs[3 * n :]
-    moves, i = [], 0
-    for a, o, b in zip(ins, outs, bufs):
-        parts = 4 if a.shape[0] > 64 else 1
-        rows = a.shape[0] // parts
-        for p in range(parts):
-            r = pl.ds(p * rows, rows)
-            moves.append(
-                (
-                    pltpu.make_async_copy(a.at[r], b.at[r], sem_in.at[i]),
-                    pltpu.make_async_copy(b.at[r], o.at[r], sem_out.at[i]),
-                )
-            )
-            i += 1
-    for get, _ in moves:
-        get.start()
-    for get, give in moves:
-        get.wait()
-        give.start()
-    for _, give in moves:
-        give.wait()
+    ins, outs, sem = refs[:n], refs[n : 2 * n], refs[2 * n]
+    moves = [pltpu.make_async_copy(a, o, sem.at[i]) for i, (a, o) in enumerate(zip(ins, outs))]
+    for m in moves:
+        m.start()
+    for m in moves:
+        m.wait()
 
 
 def shards(inputs, layer_norm_gain, w_in, w_out, pattern_in, pattern_out, out_grad):
@@ -563,7 +541,7 @@
             jax.ShapeDtypeStruct((64, 128), F32),
         ),
         in_specs=[vm(), vm(), vm(), vm(), hbm(), hbm(), vm(), vm()],
-        out_specs=(vm(), vm(), hbm(), hbm(), vm()),
+        out_specs=(vm(),) * 5,
         scratch_shapes=[
             V((2048, 512), BF),
             V((512, 2048), BF),
@@ -592,8 +570,6 @@
             V((2, 2, 2, 64, 1024), BF),
             V((2, 8, 8, 2048), BF),
             V((2, 8, 8, 2048), BF),
-            V((2048, 512), BF),
-            V((512, 2048), BF),
             V((4, 16, 128), F32),
             V((4, 16, 128), F32),
             V((8, 16, 128), F32),
@@ -602,7 +578,7 @@
             pltpu.SemaphoreType.DMA((2,)),
         ],
         compiler_params=pltpu.CompilerParams(
-            collective_id=0, has_side_effects=True, vmem_limit_bytes=67_043_328
+            collective_id=0, has_side_effects=True, vmem_limit_bytes=48 << 20
         ),
         name="ffn",
     )(
@@ -612,10 +588,10 @@
     output, grad_inputs, g_in, g_out, g_gain = pl.pallas_call(
         functools.partial(hand_over, len(out)),
         out_shape=tuple(jax.ShapeDtypeStruct(o.shape, o.dtype) for o in out),
-        in_specs=[hbm()] * len(out),
+        in_specs=[vm()] * len(out),
         out_specs=(hbm(),) * len(out),
-        scratch_shapes=[V(o.shape, o.dtype) for o in out]
-        + [pltpu.SemaphoreType.DMA((16,)), pltpu.SemaphoreType.DMA((16,))],
+        scratch_shapes=[pltpu.SemaphoreType.DMA((len(out),))],
+        compiler_params=pltpu.CompilerParams(vmem_limit_bytes=8 << 20),
         name="hand_over",
     )(*out)
     return output, grad_inputs, g_in, g_out, g_gain.reshape(8192)

time: 121 us -> 121 us (level)
  Pallas kernels: 120 us -> 115 us
  local copies, waits for them, and re-layouts: 0 us -> 3.97 us
    unnamed x0 -> x10, local copies, waits for them, and re-layouts: none -> 3.97 us
    pallas_call x1, Pallas kernels: 116 us -> 113 us  [shards(): pl.pallas_call(kernel, out_shape=(jax.ShapeDtypeStruct((8, 8192), BF), ja...]
    pallas_call x1, Pallas kernels: 4.17 us -> 2.14 us  [shards(): pl.pallas_call(functools.partial(hand_over, len(out)), out_shape=tuple((j...]
where the time goes in v5:
time: 121 us; the launch traced here: 120 us
  Pallas kernels  115 us (95%)
  local copies, waits for them, and re-layouts  3.97 us (3%)
    pallas_call x1, Pallas kernels, shards(): pl.pallas_call(kernel, out_shape=(jax.ShapeDtypeStruct((8, 8192), BF), ja...  113 us
    unnamed x10, local copies, waits for them, and re-layouts  3.97 us

profile of v5, /device:TPU:1, one launch (start us, length us, event | category | flops | bytes accessed | tf_op | source)
XLA Modules:
  0.0 120.2 jit_solution(12341383796732781204)
XLA Ops:
  0.6 0.0 copy-start
  0.6 0.7 copy-done
  1.4 0.0 copy-start.1
  1.4 0.9 copy-done.1
  2.3 0.0 copy-start.2
  2.3 0.9 copy-done.2
  3.2 0.0 copy-start.3
  3.2 0.7 copy-done.3
  3.9 0.0 copy-start.4
  3.9 0.7 copy-done.4
  4.6 113.3 %ffn.1 = (bf16[8,8192]{1,0:T(8,128)(2,1)S(1)}, bf16[8,8192]{1,0:T(8,128)(2,1)S(1)}, bf16[2048,512]{1,0:T(8,128)(2,1)S(1)}, bf16[512,2048]{1,0:T(8,128)(2,1)S(1)}, f32[64,128]{1,0:T(8,128)S(1)}) custom-call(bf16[8,8192]{1,0:T(8,128)(2,1)S(1)} %copy-done.1, f32[1,8192]{1,0:T(1,128)S(1)} %bitcast.4, f32[64,128]{1,0:T(8,128)S(1)} %bitcast.5, ...), custom_call_target="tpu_custom_call" | custom-call | tf_op jit(solution)/shard_map/ffn/pallas_call | solution.py:534
  117.9 2.1 %hand_over.1 = (bf16[8,8192]{1,0:T(8,128)(2,1)}, bf16[8,8192]{1,0:T(8,128)(2,1)}, bf16[2048,512]{1,0:T(8,128)(2,1)}, bf16[512,2048]{1,0:T(8,128)(2,1)}, f32[64,128]{1,0:T(8,128)}) custom-call(bf16[8,8192]{1,0:T(8,128)(2,1)S(1)} %get-tuple-element.15.refs_0_, bf16[8,8192]{1,0:T(8,128)(2,1)S(1)} %get-tuple-element.16.refs_1_, ...), custom_call_target="tpu_custom_call" | custom-call | tf_op jit(solution)/shard_map/hand_over/pallas_call | solution.py:588
Async XLA Ops:
  0.6 0.8 copy-start
  1.4 0.9 copy-start.1
  2.3 0.9 copy-start.2
  3.2 0.7 copy-start.3
  3.9 0.7 copy-start.4

commit v6 on v5

--- a/solution.py
+++ b/solution.py
@@ -10,6 +10,7 @@
 BF = jnp.bfloat16
 F32 = jnp.float32
 N_COPIES = 256
+SLICES = tuple((r, k) for r in range(4) for k in range(2))
 FAR_FIRST = ((1, 0, 0), (1, 1, 0), (0, 0, 1), (0, 1, 1), (1, 0, 1), (1, 1, 1), (0, 1, 0))
 
 
@@ -48,8 +49,9 @@
 
 
 def kernel(
-    x_ref, gain_ref, gain64_ref, og_ref, win_hbm, wout_hbm, pin_ref, pout_ref,
+    x_hbm, gain_hbm, gain64_hbm, og_hbm, win_hbm, wout_hbm, pin_hbm, pout_hbm,
     out_ref, gin_ref, gw1, gw2, gg_ref,
+    x_ref, gain_ref, gain64_ref, og_ref, pin_ref, pout_ref,
     win, wout, min_ref, mout_ref, normed, s0x, s0g, gx, gg,
     ar_send, ar_recv, ay_send, ay_recv, acc, act, dpre,
     rs_far, rs_half, rs_full, rs_in, rs_p,
@@ -97,6 +99,25 @@
 
     far_first = [flip(h, c, y) for h, c, y in FAR_FIRST]
 
+    loads = [
+        pltpu.make_async_copy(a, b, w_sem.at[i])
+        for i, (a, b) in enumerate(
+            (
+                (x_hbm, x_ref),
+                (gain_hbm, gain_ref),
+                (og_hbm, og_ref),
+                (pin_hbm, pin_ref),
+                (pout_hbm, pout_ref),
+                (gain64_hbm, gain64_ref),
+                (win_hbm, win),
+                (wout_hbm, wout),
+            )
+        )
+    ]
+    for c in loads:
+        c.start()
+    w_in_copy, w_out_copy = loads[6:]
+
     barrier = pltpu.get_barrier_semaphore()
     peers = [dev(xi, zi, (q + n) % 8) for n in range(1, 8)]
     peers += [dev(step(xi, n), zi, q) for n in (1, 2, 3)]
@@ -104,28 +125,29 @@
     for p in peers:
         pl.semaphore_signal(barrier, inc=1, device_id=p, device_id_type=pl.DeviceIdType.MESH)
 
-    w_in_copy = pltpu.make_async_copy(win_hbm, win, w_sem.at[0])
-    w_out_copy = pltpu.make_async_copy(wout_hbm, wout, w_sem.at[1])
-    w_in_copy.start()
-    w_out_copy.start()
-
+
+    for c in loads[:2]:
+        c.wait()
     xf = x_ref[...].astype(F32)
     cen = xf - jnp.mean(xf, axis=1, keepdims=True)
     inv = lax.rsqrt(jnp.mean(cen * cen, axis=1, keepdims=True) + 1e-05)
     nrm = (cen * inv * gain_ref[...]).astype(BF)
-    for r in range(4):
-        normed[r] = nrm[:, r * 2048 : (r + 1) * 2048]
+    for r in range(8):
+        normed[r] = nrm[:, r * 1024 : (r + 1) * 1024]
+    for c in loads[2:6]:
+        c.wait()
     pl.semaphore_wait(barrier, len(peers))
 
     def column_in(src_of, dst):
-        cs = []
-        for qq in far_first:
-            cs.append(go(src_of(qq), dst.at[q], dev(xi, zi, qq)))
-        return cs
-
-    c0x = column_in(lambda qq: normed.at[qq // 2], s0x)
-    s0x[q] = normed[row]
-    s0g[q] = og_ref[:, pl.ds(pl.multiple_of(row * 2048, 2048), 2048)]
+        return [
+            [go(src_of(qq // 2 * 2 + k), dst.at[k, q], dev(xi, zi, qq)) for qq in far_first]
+            for k in range(2)
+        ]
+
+    c0x = column_in(lambda i: normed.at[i], s0x)
+    for k in range(2):
+        s0x[k, q] = normed[row * 2 + k]
+        s0g[k, q] = og_ref[:, pl.ds(pl.multiple_of((row * 2 + k) * 1024, 1024), 1024)]
 
     lane = lax.broadcasted_iota(jnp.int32, (16, 64), 1)
     tile = lax.broadcasted_iota(jnp.int32, (16, 128), 1) + row * 8
@@ -166,11 +188,6 @@
         return st
 
     def gather(s0, g, arrived):
-        for c in arrived:
-            c.wait_recv()
-        block = s0[...].reshape(64, 2048)
-        g[0, xi, zi] = block[:, :1024]
-        g[1, xi, zi] = block[:, 1024:]
         st = colours()
 
         def one(s, off, n, v=None):
@@ -181,6 +198,9 @@
             s["s", off] = {n: one(s, off, n) for n in (1, -1)}
 
         for s in st:
+            for c in arrived[s["k"]]:
+                c.wait_recv()
+            g[s["k"], xi, zi] = s0[s["k"]].reshape(64, 1024)
             b = blk(g, s["k"], s["u0"], s["v0"])
             s["f"] = {n: go(b, b, s["to_u"](n)) for n in (1, -1)}
             both(s, 0)
@@ -378,11 +398,12 @@
             s["uw"][1].wait_recv()
             s["uw"][-1].wait_recv()
             r = r + ru_in[t, k, 0].astype(F32) + ru_in[t, k, 1].astype(F32)
-            rfin[t, :, :, k * 1024 : (k + 1) * 1024] = r.astype(BF).reshape(8, 8, 1024)
-        last[t] = [
-            go(rfin.at[t, qq], e_buf.at[t, q], dev(xi, zi, qq)) for qq in far_first
-        ]
-        e_buf[t, q] = rfin[t, q]
+            rfin[t, k] = r.astype(BF).reshape(8, 8, 1024)
+            last[t] = last.get(t, []) + [
+                go(rfin.at[t, k, qq], e_buf.at[t, k, q], dev(xi, zi, qq)) for qq in far_first
+            ]
+        for k in range(2):
+            e_buf[t, k, q] = rfin[t, k, q]
         yield
 
     ones = jnp.ones((8, 512), BF)
@@ -421,7 +442,7 @@
 
     drain(gen_x, 1)
     c0g += column_in(
-        lambda qq: og_ref.at[:, pl.ds(pl.multiple_of((qq // 2) * 2048, 2048), 2048)], s0g
+        lambda i: og_ref.at[:, pl.ds(pl.multiple_of(i * 1024, 1024), 1024)], s0g
     )
     w_in_copy.wait()
     for t in range(8):
@@ -482,9 +503,9 @@
     sx = [go(s_x.at[xi], s_x.at[xi], dev(step(xi, n), zi, q)) for n in (1, 2, 3)]
     for c in last[0]:
         c.wait_recv()
-    for r in range(4):
-        f = slice(r * 2048, (r + 1) * 2048)
-        o = e_buf[0, 2 * r].astype(F32) + e_buf[0, 2 * r + 1].astype(F32)
+    for r, k in SLICES:
+        f = slice(r * 2048 + k * 1024, r * 2048 + (k + 1) * 1024)
+        o = e_buf[0, k, 2 * r].astype(F32) + e_buf[0, k, 2 * r + 1].astype(F32)
         out_ref[:, f] = (x_ref[:, f].astype(F32) + o).astype(BF)
     drain(gen_d, 1)
     for c in sx:
@@ -507,7 +528,7 @@
     for c in last[1]:
         c.wait_recv()
     parts = [
-        e_buf[1, 2 * r].astype(F32) + e_buf[1, 2 * r + 1].astype(F32) for r in range(4)
+        e_buf[1, k, 2 * r].astype(F32) + e_buf[1, k, 2 * r + 1].astype(F32) for r, k in SLICES
     ]
     d = jnp.concatenate(parts, axis=1)
     g = d * gain_ref[...]
@@ -540,16 +561,22 @@
             jax.ShapeDtypeStruct((512, 2048), BF),
             jax.ShapeDtypeStruct((64, 128), F32),
         ),
-        in_specs=[vm(), vm(), vm(), vm(), hbm(), hbm(), vm(), vm()],
+        in_specs=[pl.BlockSpec(memory_space=pltpu.HBM)] * 8,
         out_specs=(vm(),) * 5,
         scratch_shapes=[
+            V((8, 8192), BF),
+            V((1, 8192), F32),
+            V((64, 128), F32),
+            V((8, 8192), BF),
+            V((16, 64), jnp.int32),
+            V((32, 32), jnp.int32),
             V((2048, 512), BF),
             V((512, 2048), BF),
             V((8, 512), F32),
             V((2, 2048), F32),
-            V((4, 8, 2048), BF),
-            V((8, 8, 2048), BF),
-            V((8, 8, 2048), BF),
+            V((8, 8, 1024), BF),
+            V((2, 8, 8, 1024), BF),
+            V((2, 8, 8, 1024), BF),
             V((2, 4, 4, 64, 1024), BF),
             V((2, 4, 4, 64, 1024), BF),
             V((2, 2, 256, 512), BF),
@@ -568,22 +595,27 @@
             V((2, 2, 2, 32, 1024), BF),
             V((2, 2, 2, 64, 1024), BF),
             V((2, 2, 2, 64, 1024), BF),
-            V((2, 8, 8, 2048), BF),
-            V((2, 8, 8, 2048), BF),
+            V((2, 2, 8, 8, 1024), BF),
+            V((2, 2, 8, 8, 1024), BF),
             V((4, 16, 128), F32),
             V((4, 16, 128), F32),
             V((8, 16, 128), F32),
             pltpu.SemaphoreType.DMA((N_COPIES,)),
             pltpu.SemaphoreType.DMA((N_COPIES,)),
-            pltpu.SemaphoreType.DMA((2,)),
+            pltpu.SemaphoreType.DMA((8,)),
         ],
         compiler_params=pltpu.CompilerParams(
             collective_id=0, has_side_effects=True, vmem_limit_bytes=48 << 20
         ),
         name="ffn",
     )(
-        inputs, layer_norm_gain.reshape(1, 8192), layer_norm_gain.reshape(64, 128), out_grad,
-        w_in, w_out, pattern_in.T, pattern_out,
+        *(
+            pltpu.with_memory_space_constraint(a, pltpu.HBM)
+            for a in (
+                inputs, layer_norm_gain.reshape(1, 8192), layer_norm_gain.reshape(64, 128),
+                out_grad, w_in, w_out, pattern_in.T, pattern_out,
+            )
+        )
     )
     output, grad_inputs, g_in, g_out, g_gain = pl.pallas_call(
         functools.partial(hand_over, len(out)),

time: 121 us -> 117 us (0.967)
  local copies, waits for them, and re-layouts: 3.97 us -> 0 us
    unnamed x10 -> x0, local copies, waits for them, and re-layouts: 3.97 us -> none
where the time goes in v6:
time: 117 us
  Pallas kernels  116 us (99%)
    pallas_call x1, Pallas kernels, shards(): pl.pallas_call(kernel, out_shape=(jax.ShapeDtypeStruct((8, 8192), BF), ja...  114 us

profile of v6, /device:TPU:1, one launch (start us, length us, event | category | flops | bytes accessed | tf_op | source)
XLA Modules:
  0.0 116.6 jit_solution(5177046119285937354)
XLA Ops:
  0.6 113.6 %ffn.1 = (bf16[8,8192]{1,0:T(8,128)(2,1)S(1)}, bf16[8,8192]{1,0:T(8,128)(2,1)S(1)}, bf16[2048,512]{1,0:T(8,128)(2,1)S(1)}, bf16[512,2048]{1,0:T(8,128)(2,1)S(1)}, f32[64,128]{1,0:T(8,128)S(1)}) custom-call(bf16[8,8192]{1,0:T(8,128)(2,1)} %x_hbm.1, f32[1,8192]{1,0:T(1,128)} %bitcast.4, f32[64,128]{1,0:T(8,128)} %bitcast.5, bf16[8,8192]{1,0:T(8,128)(2,1)} %og_hbm.1, ...), custom_call_target="tpu_custom_call" | custom-call | tf_op jit(solution)/shard_map/ffn/pallas_call | solution.py:555
  114.2 2.1 %hand_over.1 = (bf16[8,8192]{1,0:T(8,128)(2,1)}, bf16[8,8192]{1,0:T(8,128)(2,1)}, bf16[2048,512]{1,0:T(8,128)(2,1)}, bf16[512,2048]{1,0:T(8,128)(2,1)}, f32[64,128]{1,0:T(8,128)}) custom-call(bf16[8,8192]{1,0:T(8,128)(2,1)S(1)} %get-tuple-element.15.refs_0_, bf16[8,8192]{1,0:T(8,128)(2,1)S(1)} %get-tuple-element.16.refs_1_, ...), custom_call_target="tpu_custom_call" | custom-call | tf_op jit(solution)/shard_map/hand_over/pallas_call | solution.py:620

commit v7 on v6

--- a/solution.py
+++ b/solution.py
@@ -187,11 +187,29 @@
             )
         return st
 
-    def gather(s0, g, arrived):
+    def gather(s0, g, arrived, lean):
         st = colours()
 
-        def one(s, off, n, v=None):
-            b = blk(g, s["k"], step(s["u0"], off), s["v0"] if v is None else v)
+        def view(s, u_off, v_off, rows=pl.ds(0, 64), lanes=None):
+            b = blk(g, s["k"], step(s["u0"], u_off), step(s["v0"], v_off))
+            if not lean:
+                return b.at[rows]
+            return b.at[rows, pl.ds(pl.multiple_of(yl * 128, 128), 896) if lanes is None else lanes]
+
+        def push(s, u_off, v_off):
+            if lean:
+                b = view(s, u_off, v_off, lanes=pl.ds(pl.multiple_of(yl * 896, 128), 128))
+                s["p"][u_off, v_off] = go(b, b, dev(xi, zi, flip(0, 0, 1)))
+
+        def pushed(offs):
+            if lean:
+                for s in st:
+                    for key, c in s["p"].items():
+                        if key[1 - s["k"]] in offs:
+                            c.wait_recv()
+
+        def one(s, off, n, v_off=0):
+            b = view(s, off, v_off)
             return go(b, b, s["to_v"](n))
 
         def both(s, off):
@@ -201,7 +219,8 @@
             for c in arrived[s["k"]]:
                 c.wait_recv()
             g[s["k"], xi, zi] = s0[s["k"]].reshape(64, 1024)
-            b = blk(g, s["k"], s["u0"], s["v0"])
+            b = view(s, 0, 0)
+            s["p"] = {}
             s["f"] = {n: go(b, b, s["to_u"](n)) for n in (1, -1)}
             both(s, 0)
             s["f2"], s["s2"] = {}, {}
@@ -209,15 +228,16 @@
         for n in (1, -1):
             for s in st:
                 s["f"][n].wait_recv()
-                b = blk(g, s["k"], step(s["u0"], -n), s["v0"])
-                part = b.at[pl.ds(0, 32)] if n == 1 else b.at[pl.ds(32, 32)]
+                part = view(s, -n, 0, pl.ds(0 if n == 1 else 32, 32))
                 s["f2"][n] = go(part, part, s["to_u"](n))
                 both(s, -n)
+                push(s, -n, 0)
             yield
 
         def relay(s, off, n):
             s["s", off][n].wait_recv()
-            s["s2"][off] = one(s, off, n, step(s["v0"], -n))
+            s["s2"][off] = one(s, off, n, -n)
+            push(s, off, -n)
 
         for s in st:
             relay(s, 0, 1)
@@ -226,8 +246,10 @@
             s["f2"][1].wait_recv()
             s["f2"][-1].wait_recv()
             both(s, 2)
+            push(s, 2, 0)
         for s in st:
             s["s", 0][-1].wait_recv()
+            push(s, 0, 1)
         yield
         for off in (-1, 1, 2):
             n = 1 if off == 1 else -1
@@ -235,19 +257,25 @@
                 relay(s, off, n)
             for s in st:
                 s["s", off][-n].wait_recv()
+                push(s, off, n)
             yield
         for off in (0, -1, 1, 2):
             for s in st:
                 s["s2"][off].wait_recv()
+                push(s, off, 2)
+            if off == -1:
+                pushed((0, -1))
+            if off == 2:
+                pushed((1, 2))
             yield
 
     def drain(g, n):
         for _ in range(n):
             next(g, None)
 
-    gen_x = gather(s0x, gx, c0x)
+    gen_x = gather(s0x, gx, c0x, True)
     c0g = []
-    gen_g = gather(s0g, gg, c0g)
+    gen_g = gather(s0g, gg, c0g, False)
 
     def partial(g, w, nt, xx):
         a = g[0, xx].reshape(256, 1024)
@@ -473,9 +501,9 @@
     drain(gen_o, 1)
     drain(gen_g, 2)
     da0 = row_other(1, 0)
-    drain(gen_o, 1)
     row_mine(1, 0)
     db0 = row_add(1, 0, da0)
+    drain(gen_o, 1)
     drain(gen_g, 2)
     da1 = row_other(1, 1)
     row_mine(1, 1)
@@ -485,22 +513,24 @@
     dc0 = row_dpre(0, db0)
     drain(gen_o, 1)
     grad_out_tiles(0, 2, 4)
+    grad_out_tiles(1, 0, 2)
     drain(gen_o, 1)
     dc1 = row_dpre(1, db1)
+    grad_out_tiles(1, 2, 4)
     dc0.wait_recv()
     dc1.wait_recv()
     gen_d = scatter(1)
     drain(gen_d, 1)
+    grad_in_tiles(0, 0, 2)
     drain(gen_o, 1)
     drain(gen_d, 1)
-    grad_out_tiles(1, 0, 2)
+    grad_in_tiles(0, 2, 3)
     drain(gen_d, 1)
-    grad_out_tiles(1, 2, 4)
-    drain(gen_d, 1)
-    grad_in_tiles(0, 0, 4)
+    grad_in_tiles(0, 3, 4)
     drain(gen_d, 1)
     grad_in_tiles(1, 0, 4)
     sx = [go(s_x.at[xi], s_x.at[xi], dev(step(xi, n), zi, q)) for n in (1, 2, 3)]
+    drain(gen_d, 1)
     for c in last[0]:
         c.wait_recv()
     for r, k in SLICES:

time: 117 us -> 121 us (1.034)
  Pallas kernels: 116 us -> 120 us
    pallas_call x1, Pallas kernels: 114 us -> 118 us  [shards(): pl.pallas_call(kernel, out_shape=(jax.ShapeDtypeStruct((8, 8192), BF), ja...]
where the time goes in v7:
time: 121 us; the launch traced here: 120 us
  Pallas kernels  120 us (99%)
    pallas_call x1, Pallas kernels, shards(): pl.pallas_call(kernel, out_shape=(jax.ShapeDtypeStruct((8, 8192), BF), ja...  118 us

profile of v7, /device:TPU:1, one launch (start us, length us, event | category | flops | bytes accessed | tf_op | source)
XLA Modules:
  0.0 120.5 jit_solution(1593555970303134059)
XLA Ops:
  0.6 117.5 %ffn.1 = (bf16[8,8192]{1,0:T(8,128)(2,1)S(1)}, bf16[8,8192]{1,0:T(8,128)(2,1)S(1)}, bf16[2048,512]{1,0:T(8,128)(2,1)S(1)}, bf16[512,2048]{1,0:T(8,128)(2,1)S(1)}, f32[64,128]{1,0:T(8,128)S(1)}) custom-call(bf16[8,8192]{1,0:T(8,128)(2,1)} %x_hbm.1, f32[1,8192]{1,0:T(1,128)} %bitcast.4, f32[64,128]{1,0:T(8,128)} %bitcast.5, bf16[8,8192]{1,0:T(8,128)(2,1)} %og_hbm.1, ...), custom_call_target="tpu_custom_call" | custom-call | tf_op jit(solution)/shard_map/ffn/pallas_call | solution.py:585
  118.2 2.1 %hand_over.1 = (bf16[8,8192]{1,0:T(8,128)(2,1)}, bf16[8,8192]{1,0:T(8,128)(2,1)}, bf16[2048,512]{1,0:T(8,128)(2,1)}, bf16[512,2048]{1,0:T(8,128)(2,1)}, f32[64,128]{1,0:T(8,128)}) custom-call(bf16[8,8192]{1,0:T(8,128)(2,1)S(1)} %get-tuple-element.15.refs_0_, bf16[8,8192]{1,0:T(8,128)(2,1)S(1)} %get-tuple-element.16.refs_1_, ...), custom_call_target="tpu_custom_call" | custom-call | tf_op jit(solution)/shard_map/hand_over/pallas_call | solution.py:650

commit v8 on v6

--- a/solution.py
+++ b/solution.py
@@ -147,24 +147,6 @@
     c0x = column_in(lambda i: normed.at[i], s0x)
     for k in range(2):
         s0x[k, q] = normed[row * 2 + k]
-        s0g[k, q] = og_ref[:, pl.ds(pl.multiple_of((row * 2 + k) * 1024, 1024), 1024)]
-
-    lane = lax.broadcasted_iota(jnp.int32, (16, 64), 1)
-    tile = lax.broadcasted_iota(jnp.int32, (16, 128), 1) + row * 8
-    for h in range(2):
-        rows = jnp.max(jnp.where(lane == col * 2 + h, pin_ref[...], -1), axis=1, keepdims=True)
-        kept = jnp.max(jnp.where(rows == tile, 1.0, 0.0), axis=0, keepdims=True)
-        for t in range(8):
-            min_ref[t : t + 1, h * 256 : (h + 1) * 256] = jnp.broadcast_to(
-                kept[:, t : t + 1], (1, 256)
-            )
-    pout = pout_ref[pl.ds(pl.multiple_of(row * 8, 8), 8), :]
-    for h in range(2):
-        kept = jnp.max(jnp.where(pout == col * 2 + h, 1.0, 0.0), axis=1, keepdims=True)
-        for t in range(8):
-            mout_ref[h : h + 1, t * 256 : (t + 1) * 256] = jnp.broadcast_to(
-                kept[t : t + 1], (1, 256)
-            )
 
     def blk(g, k, u, v):
         return g.at[0, v, u] if k == 0 else g.at[1, u, v]
@@ -444,14 +426,32 @@
     c0g += column_in(
         lambda i: og_ref.at[:, pl.ds(pl.multiple_of(i * 1024, 1024), 1024)], s0g
     )
+    for k in range(2):
+        s0g[k, q] = og_ref[:, pl.ds(pl.multiple_of((row * 2 + k) * 1024, 1024), 1024)]
+    lane = lax.broadcasted_iota(jnp.int32, (16, 64), 1)
+    tile = lax.broadcasted_iota(jnp.int32, (16, 128), 1) + row * 8
+    for h in range(2):
+        rows = jnp.max(jnp.where(lane == col * 2 + h, pin_ref[...], -1), axis=1, keepdims=True)
+        kept = jnp.max(jnp.where(rows == tile, 1.0, 0.0), axis=0, keepdims=True)
+        for t in range(8):
+            min_ref[t : t + 1, h * 256 : (h + 1) * 256] = jnp.broadcast_to(
+                kept[:, t : t + 1], (1, 256)
+            )
     w_in_copy.wait()
     for t in range(8):
         win[t * 256 : (t + 1) * 256] = win[t * 256 : (t + 1) * 256] * min_ref[t : t + 1].astype(BF)
+    drain(gen_x, 7)
+    drain(gen_g, 1)
+    pout = pout_ref[pl.ds(pl.multiple_of(row * 8, 8), 8), :]
+    for h in range(2):
+        kept = jnp.max(jnp.where(pout == col * 2 + h, 1.0, 0.0), axis=1, keepdims=True)
+        for t in range(8):
+            mout_ref[h : h + 1, t * 256 : (t + 1) * 256] = jnp.broadcast_to(
+                kept[t : t + 1], (1, 256)
+            )
     w_out_copy.wait()
     for t in range(2):
         wout[t * 256 : (t + 1) * 256] = wout[t * 256 : (t + 1) * 256] * mout_ref[t : t + 1].astype(BF)
-    drain(gen_x, 7)
-    drain(gen_g, 1)
     drain(gen_x, 2)
     ca0 = row_other(0, 0)
     row_mine(0, 0)
@@ -473,9 +473,9 @@
     drain(gen_o, 1)
     drain(gen_g, 2)
     da0 = row_other(1, 0)
-    drain(gen_o, 1)
     row_mine(1, 0)
     db0 = row_add(1, 0, da0)
+    drain(gen_o, 1)
     drain(gen_g, 2)
     da1 = row_other(1, 1)
     row_mine(1, 1)
@@ -485,22 +485,24 @@
     dc0 = row_dpre(0, db0)
     drain(gen_o, 1)
     grad_out_tiles(0, 2, 4)
+    grad_out_tiles(1, 0, 2)
     drain(gen_o, 1)
     dc1 = row_dpre(1, db1)
+    grad_out_tiles(1, 2, 4)
     dc0.wait_recv()
     dc1.wait_recv()
     gen_d = scatter(1)
     drain(gen_d, 1)
+    grad_in_tiles(0, 0, 2)
     drain(gen_o, 1)
     drain(gen_d, 1)
-    grad_out_tiles(1, 0, 2)
+    grad_in_tiles(0, 2, 3)
     drain(gen_d, 1)
-    grad_out_tiles(1, 2, 4)
-    drain(gen_d, 1)
-    grad_in_tiles(0, 0, 4)
+    grad_in_tiles(0, 3, 4)
     drain(gen_d, 1)
     grad_in_tiles(1, 0, 4)
     sx = [go(s_x.at[xi], s_x.at[xi], dev(step(xi, n), zi, q)) for n in (1, 2, 3)]
+    drain(gen_d, 1)
     for c in last[0]:
         c.wait_recv()
     for r, k in SLICES:
@@ -512,19 +514,19 @@
         c.wait_recv()
     s_z[zi] = (s_x[0] + s_x[1]) + (s_x[2] + s_x[3])
     sz = [go(s_z.at[zi], s_z.at[zi], dev(xi, step(zi, n), q)) for n in (1, 2, 3)]
-    drain(gen_d, 1)
     for c in sz:
         c.wait_recv()
     s_c[q] = (s_z[0] + s_z[1]) + (s_z[2] + s_z[3])
-    sc = [go(s_c.at[q], s_c.at[q], dev(xi, zi, (q + n) % 8)) for n in range(1, 8)]
-    for c in sc:
-        c.wait_recv()
-    for r in range(4):
-        gg_ref[r * 16 : (r + 1) * 16] = (s_c[2 * r] + s_c[2 * r + 1]) / gain64_ref[r * 16 : (r + 1) * 16]
+    sc = [go(s_c.at[q], s_c.at[q], dev(xi, zi, qq)) for qq in far_first]
     xf = x_ref[...].astype(F32)
     cen = xf - jnp.mean(xf, axis=1, keepdims=True)
     inv = lax.rsqrt(jnp.mean(cen * cen, axis=1, keepdims=True) + 1e-05)
     hat = cen * inv
+    drain(gen_d, 1)
+    for c in sc:
+        c.wait_recv()
+    for r in range(4):
+        gg_ref[r * 16 : (r + 1) * 16] = (s_c[2 * r] + s_c[2 * r + 1]) / gain64_ref[r * 16 : (r + 1) * 16]
     for c in last[1]:
         c.wait_recv()
     parts = [

time: 117 us -> 116 us (level)
  no operation moved by 1% of the time
where the time goes in v8:
time: 116 us
  Pallas kernels  115 us (99%)
    pallas_call x1, Pallas kernels, shards(): pl.pallas_call(kernel, out_shape=(jax.ShapeDtypeStruct((8, 8192), BF), ja...  113 us

profile of v8, /device:TPU:1, one launch (start us, length us, event | category | flops | bytes accessed | tf_op | source)
XLA Modules:
  0.0 116.3 jit_solution(5098997974803118028)
XLA Ops:
  0.6 113.3 %ffn.1 = (bf16[8,8192]{1,0:T(8,128)(2,1)S(1)}, bf16[8,8192]{1,0:T(8,128)(2,1)S(1)}, bf16[2048,512]{1,0:T(8,128)(2,1)S(1)}, bf16[512,2048]{1,0:T(8,128)(2,1)S(1)}, f32[64,128]{1,0:T(8,128)S(1)}) custom-call(bf16[8,8192]{1,0:T(8,128)(2,1)} %x_hbm.1, f32[1,8192]{1,0:T(1,128)} %bitcast.4, f32[64,128]{1,0:T(8,128)} %bitcast.5, bf16[8,8192]{1,0:T(8,128)(2,1)} %og_hbm.1, ...), custom_call_target="tpu_custom_call" | custom-call | tf_op jit(solution)/shard_map/ffn/pallas_call | solution.py:557
  113.9 2.1 %hand_over.1 = (bf16[8,8192]{1,0:T(8,128)(2,1)}, bf16[8,8192]{1,0:T(8,128)(2,1)}, bf16[2048,512]{1,0:T(8,128)(2,1)}, bf16[512,2048]{1,0:T(8,128)(2,1)}, f32[64,128]{1,0:T(8,128)}) custom-call(bf16[8,8192]{1,0:T(8,128)(2,1)S(1)} %get-tuple-element.15.refs_0_, bf16[8,8192]{1,0:T(8,128)(2,1)S(1)} %get-tuple-element.16.refs_1_, ...), custom_call_target="tpu_custom_call" | custom-call | tf_op jit(solution)/shard_map/hand_over/pallas_call | solution.py:622

commit v9 on v8

--- a/solution.py
+++ b/solution.py
@@ -134,8 +134,6 @@
     nrm = (cen * inv * gain_ref[...]).astype(BF)
     for r in range(8):
         normed[r] = nrm[:, r * 1024 : (r + 1) * 1024]
-    for c in loads[2:6]:
-        c.wait()
     pl.semaphore_wait(barrier, len(peers))
 
     def column_in(src_of, dst):
@@ -147,6 +145,8 @@
     c0x = column_in(lambda i: normed.at[i], s0x)
     for k in range(2):
         s0x[k, q] = normed[row * 2 + k]
+    for c in loads[2:6]:
+        c.wait()
 
     def blk(g, k, u, v):
         return g.at[0, v, u] if k == 0 else g.at[1, u, v]
@@ -185,8 +185,9 @@
             g[s["k"], xi, zi] = s0[s["k"]].reshape(64, 1024)
             b = blk(g, s["k"], s["u0"], s["v0"])
             s["f"] = {n: go(b, b, s["to_u"](n)) for n in (1, -1)}
+            s["f2"], s["s2"] = {}, {}
+        for s in st:
             both(s, 0)
-            s["f2"], s["s2"] = {}, {}
         yield
         for n in (1, -1):
             for s in st:

time: 116 us -> 115 us (level)
  no operation moved by 1% of the time
where the time goes in v9:
time: 115 us
  Pallas kernels  114 us (99%)
    pallas_call x1, Pallas kernels, shards(): pl.pallas_call(kernel, out_shape=(jax.ShapeDtypeStruct((8, 8192), BF), ja...  112 us

profile of v9, /device:TPU:1, one launch (start us, length us, event | category | flops | bytes accessed | tf_op | source)
XLA Modules:
  0.0 115.1 jit_solution(11389465156017564753)
XLA Ops:
  0.6 112.2 %ffn.1 = (bf16[8,8192]{1,0:T(8,128)(2,1)S(1)}, bf16[8,8192]{1,0:T(8,128)(2,1)S(1)}, bf16[2048,512]{1,0:T(8,128)(2,1)S(1)}, bf16[512,2048]{1,0:T(8,128)(2,1)S(1)}, f32[64,128]{1,0:T(8,128)S(1)}) custom-call(bf16[8,8192]{1,0:T(8,128)(2,1)} %x_hbm.1, f32[1,8192]{1,0:T(1,128)} %bitcast.4, f32[64,128]{1,0:T(8,128)} %bitcast.5, bf16[8,8192]{1,0:T(8,128)(2,1)} %og_hbm.1, ...), custom_call_target="tpu_custom_call" | custom-call | tf_op jit(solution)/shard_map/ffn/pallas_call | solution.py:558
  112.8 2.1 %hand_over.1 = (bf16[8,8192]{1,0:T(8,128)(2,1)}, bf16[8,8192]{1,0:T(8,128)(2,1)}, bf16[2048,512]{1,0:T(8,128)(2,1)}, bf16[512,2048]{1,0:T(8,128)(2,1)}, f32[64,128]{1,0:T(8,128)}) custom-call(bf16[8,8192]{1,0:T(8,128)(2,1)S(1)} %get-tuple-element.15.refs_0_, bf16[8,8192]{1,0:T(8,128)(2,1)S(1)} %get-tuple-element.16.refs_1_, ...), custom_call_target="tpu_custom_call" | custom-call | tf_op jit(solution)/shard_map/hand_over/pallas_call | solution.py:623
